TPU v7x, 32 devices: a whole 2x2x4 slice. The times are simulated.
32 devices in a mesh: gx: 8 (over y, x, core), gy: 4 (over z).
Axes of the slice: x: 2, y: 2, z: 4, core: 2. Of those that a mesh axis runs over, the one named last changes fastest.
Arguments:
- composition: float32 [53, 262144], P(None, ('gx', 'gy')), may hold values from -6 to 6
- particle_mass: float32 [262144], P(('gx', 'gy')), may hold values from 0.3 to 3
- particle_cell: int32 [2, 262144], P(None, ('gx', 'gy')), may hold values from 0 to 511, as said below
- particle_level: int32 [262144], P(('gx', 'gy')), may hold values from 0 to 2, as said below
- les_mean: float32 [53, 32, 512], P(None, 'gx', 'gy'), may hold values from -6 to 6
- mix_rate: float32 [32, 512], P('gx', 'gy'), may hold values from 0.1 to 3
- rate_matrix: float32 [3, 53, 53], replicated, may hold values from -0.875 to 0.875
- implicit_map: float32 [3, 53, 53], replicated, may hold values from -0.875 to 0.875
Outputs:
- updated: float32 [53, 262144], P(None, ('gx', 'gy'))
- cell_means: float32 [53, 32, 512], P(None, 'gx', 'gy')
Inputs may be any that keep to these rules, and one draw needn't show every extreme that they name: `particle_cell`: row 0 is below 32 and row 1 below 512. With the cells split into blocks of 4 x 128 cells in device order (streamwise block index major), every particle's cell lies within 2 cells, in each grid direction, of the block of the device that holds the particle; the distance 2 is reached on every side that has a neighbouring block. `particle_level`: the share of full-mechanism particles differs from device to device, from none to all.
All inputs are finite; a program needn't handle non-finite values.
Results may differ from a plain program's by a relative error of at most 0.0001.
Values sent between devices are 32-bit elements; how exact they have to be, the bound alone decides.
A program may use at most 64 MiB of HBM per device.

v0:
```python
import functools

import jax
import jax.numpy as jnp
from jax import lax
from jax.experimental import pallas as pl
from jax.experimental.pallas import tpu as pltpu
from jax.sharding import PartitionSpec as P

NS_LOW = 21
NS_MID = 24
R = 2
W = 2 * R
HALF = 64
ROWS = 56
LANES = 128

prior_weight = 16.0
chem_step = 0.5
BF = jnp.bfloat16
F32 = jnp.float32
MESH = pl.DeviceIdType.MESH


def halves(value):
    high = value.astype(BF)
    return high, (value - high.astype(F32)).astype(BF)


def roll(value, shift):
    return pltpu.roll(value, shift % value.shape[1], 1)


def positions(cell, block_x, block_y):
    local_x = cell[0:1] - (lax.axis_index("gx") * block_x - R)
    local_y = cell[1:2] - (lax.axis_index("gy") * block_y - R)
    low_rim = local_y < W
    on_rim = low_rim | (local_y >= block_y)
    rim = jnp.where(low_rim, local_y, local_y - block_y + (block_x + 2 * R) * W) + local_x * W
    return local_x, jnp.where(on_rim, -1, local_y - R), jnp.where(on_rim, rim, -1)


def one_hot(place, rows):
    sub = lax.broadcasted_iota(jnp.int32, (rows, place.shape[1]), 0)
    same = sub.astype(F32).astype(BF) == jnp.broadcast_to(
        place.astype(F32), (rows, place.shape[1])
    ).astype(BF)
    return jnp.where(same, jnp.ones((), BF), jnp.zeros((), BF))


def sums_kernel(
    counts, steps, chunk, block_x, block_y, comp, mass, cell, les, rate, table,
    hot, hot_rim, weighted, split, acc, acc_rim,
    send, prior, from_x, from_y, from_xy, send_main, recv_main, send_rim, recv_rim,
):
    species = comp.shape[0]
    span_x = block_x + 2 * R
    side_size = span_x * W
    gx, gy = lax.axis_index("gx"), lax.axis_index("gy")
    index = pl.program_id(0)
    has = {
        -1: (gx > 0, gy > 0),
        1: (gx < counts[0] - 1, gy < counts[1] - 1),
        0: (True, True),
    }
    others = [(dx, dy) for dx in (-1, 0, 1) for dy in (-1, 0, 1) if (dx, dy) != (0, 0)]
    lane = lax.broadcasted_iota(jnp.int32, (ROWS, LANES), 1)
    row = lax.broadcasted_iota(jnp.int32, (ROWS, LANES), 0)
    inside = (lane >= R) & (lane < block_y - R)

    def present(dx, dy):
        return jnp.logical_and(has[dx][0], has[dy][1])

    def landing(dx, dy):
        if dy == 0:
            return from_x.at[(dx + 1) // 2, W]
        if dx == 0:
            return from_y.at[(dy + 1) // 2]
        return from_xy.at[(dx + 1) // 2, (dy + 1) // 2]

    def main_copy(dx):
        first = 0 if dx < 0 else block_x
        return pltpu.make_async_remote_copy(
            src_ref=send.at[pl.ds(first, W)],
            dst_ref=from_x.at[(1 - dx) // 2, pl.ds(0, W)],
            send_sem=send_main.at[(dx + 1) // 2],
            recv_sem=recv_main.at[(1 - dx) // 2],
            device_id=(gx + dx, gy),
            device_id_type=MESH,
        )

    def rim_copy(k, dx, dy):
        return pltpu.make_async_remote_copy(
            src_ref=send.at[span_x],
            dst_ref=landing(-dx, -dy),
            send_sem=send_rim.at[k],
            recv_sem=recv_rim.at[len(others) - 1 - k],
            device_id=(gx + dx, gy + dy),
            device_id_type=MESH,
        )

    def main_arrival(dx):
        return pltpu.make_async_remote_copy(
            src_ref=send.at[pl.ds(0, W)],
            dst_ref=from_x.at[(dx + 1) // 2, pl.ds(0, W)],
            send_sem=send_main.at[(dx + 1) // 2],
            recv_sem=recv_main.at[(dx + 1) // 2],
            device_id=(gx + dx, gy),
            device_id_type=MESH,
        )

    def rim_arrival(k, dx, dy):
        return pltpu.make_async_remote_copy(
            src_ref=send.at[span_x],
            dst_ref=landing(dx, dy),
            send_sem=send_rim.at[k],
            recv_sem=recv_rim.at[k],
            device_id=(gx + dx, gy + dy),
            device_id_type=MESH,
        )

    def masked(local_x, pairs, value):
        parts = []
        for pair in pairs:
            keep = jnp.broadcast_to(local_x // 2 == pair, (16, chunk))
            keep = jnp.where(keep, 1.0, 0.0).astype(BF)
            parts.append(value * jnp.concatenate([keep] * (2 * ROWS // 16), 0))
        return jnp.concatenate(parts, 0)

    def accumulate(total, left, right):
        total[...] += lax.dot_general(
            left, right, (((1,), (1,)), ((), ())), preferred_element_type=F32
        )

    def tile(pair, parity):
        at = (pair % (span_x // 4)) * 2 * ROWS
        cols = slice(parity * block_y, (parity + 1) * block_y)
        return acc[at : at + ROWS, cols] + acc[at + ROWS : at + 2 * ROWS, cols]

    def ready(first, last):
        for t in range(first, last):
            value = tile(t // 2, t % 2)
            if R <= t < R + block_x:
                value = value + jnp.where(inside, prior[t - R], 0.0)
            send[t] = value

    half = span_x // 4
    barrier = pltpu.get_barrier_semaphore()

    @pl.when(index == 0)
    def _():
        for dx, dy in others:
            @pl.when(present(dx, dy))
            def _():
                pl.semaphore_signal(
                    barrier, inc=1, device_id=(gx + dx, gy + dy), device_id_type=MESH
                )
        acc[...] = jnp.zeros_like(acc)
        acc_rim[...] = jnp.zeros_like(acc_rim)
        weighted[...] = jnp.zeros_like(weighted)
        prior[...] = jnp.zeros_like(prior)
        for x in range(block_x):
            prior[x, 0:species, :] = prior_weight * les[:, x, :]
            prior[x, species : species + 1, :] = jnp.full((1, block_y), prior_weight, F32)
            prior[x, species + 1 : species + 2, :] = 1.0 - jnp.exp(-rate[x : x + 1, :])
        for dx in (-1, 1):
            @pl.when(jnp.logical_not(has[dx][0]))
            def _():
                from_x[(dx + 1) // 2] = jnp.zeros((W + 1, ROWS, LANES), F32)
        for dx, dy in others:
            if dy != 0:
                @pl.when(jnp.logical_not(present(dx, dy)))
                def _():
                    landing(dx, dy)[...] = jnp.zeros((ROWS, LANES), F32)

    @pl.when(index < steps)
    def _():
        weighted[0:species, :] = comp[...] * mass[...]
        weighted[species : species + 1, :] = mass[...]
        value = weighted[...]
        high = value.astype(BF).astype(F32)
        both = jnp.concatenate([high, value - high], 0).astype(BF)
        split[index] = both
        local_x, inner, rim = positions(cell[...], block_x, block_y)
        column = jnp.where(inner < 0, -1, inner + (local_x % 2) * block_y)
        hot[index] = one_hot(column, 2 * block_y)
        hot_rim[...] = one_hot(rim, HALF)
        accumulate(acc, masked(local_x, range(half), both), hot[index])
        acc_rim[:, 0:HALF] += lax.dot_general(
            both, hot_rim[...], (((1,), (1,)), ((), ())), preferred_element_type=F32
        )

    @pl.when(index == steps - 1)
    def _():
        ready(0, W)
        rim_sum = acc_rim[0:ROWS, :] + acc_rim[ROWS:, :]
        for x in range(block_x):
            t = x + R
            low_at, high_at = t * W + R, side_size + t * W
            low, high = roll(prior[x], low_at), roll(prior[x], high_at + R)
            rim_sum += jnp.where((lane >= low_at) & (lane < low_at + R), low, 0.0)
            rim_sum += jnp.where((lane >= high_at) & (lane < high_at + R), high, 0.0)
        send[span_x] = rim_sum
        acc[...] = jnp.zeros_like(acc)
        number = (1 + (gx > 0).astype(jnp.int32) + (gx < counts[0] - 1).astype(jnp.int32)) * (
            1 + (gy > 0).astype(jnp.int32) + (gy < counts[1] - 1).astype(jnp.int32)
        ) - 1
        pl.semaphore_wait(barrier, number)

        @pl.when(has[-1][0])
        def _():
            main_copy(-1).start()

        for k, (dx, dy) in enumerate(others):
            @pl.when(present(dx, dy))
            def _():
                rim_copy(k, dx, dy).start()

    @pl.when(index >= steps)
    def _():
        at = index - steps
        local_x, _, _ = positions(cell[...], block_x, block_y)
        accumulate(acc, masked(local_x, range(half, 2 * half), split[at]), hot[at])

    @pl.when(index == 2 * steps - 1)
    def _():
        ready(W, span_x)

        @pl.when(has[1][0])
        def _():
            main_copy(1).start()

        for k, (dx, dy) in enumerate(others):
            @pl.when(present(dx, dy))
            def _():
                rim_arrival(k, dx, dy).wait_recv()

        @pl.when(has[1][0])
        def _():
            main_arrival(1).wait_recv()

        def finish(total):
            total_mass = total[species : species + 1, :]
            weight = jnp.where(total_mass > 0.0, total_mass, 1.0)
            weight = jnp.broadcast_to(weight, total.shape)
            return total / jnp.where(row < species, weight, 1.0)

        low_side = lane < side_size
        place_x = jnp.where(low_side, lane, lane - side_size)
        used = lane < 2 * side_size
        behind = used & (place_x < 2 * R * W)
        ahead = used & (place_x >= block_x * W)
        total = send[span_x]
        for dx, dy in others:
            mask = used if dx == 0 else behind if dx < 0 else ahead
            if dy != 0:
                mask = mask & (low_side if dy < 0 else jnp.logical_not(low_side))
            shift = dx * block_x * W + dy * side_size
            total = total + jnp.where(mask, roll(landing(dx, dy)[...], shift), 0.0)
        rim_value = finish(total)
        table[span_x] = rim_value

        def close(t):
            total = send[t]
            if t < W:
                total = total + from_x[0, t]
            if t >= block_x:
                total = total + from_x[1, t - block_x]
            value = finish(total)
            if R <= t < R + block_x:
                low_at, high_at = t * W + R, side_size + t * W
                value = jnp.where(lane < R, roll(rim_value, -low_at), value)
                value = jnp.where(
                    lane >= block_y - R, roll(rim_value, block_y - R - high_at), value
                )
            table[t] = value

        for t in range(W, span_x):
            close(t)

        @pl.when(has[-1][0])
        def _():
            main_arrival(-1).wait_recv()

        for t in range(W):
            close(t)
        for k, (dx, dy) in enumerate(others):
            @pl.when(present(dx, dy))
            def _():
                rim_copy(k, dx, dy).wait_send()
        for dx in (-1, 1):
            @pl.when(has[dx][0])
            def _():
                main_copy(dx).wait_send()


def stack_levels(target, plain, matrices):
    species = matrices.shape[1]
    plain[...] = jnp.zeros_like(plain)
    plain[0:species, 0:species] = matrices[2]
    plain[HALF : HALF + NS_MID, 0:NS_MID] = matrices[1, 0:NS_MID, 0:NS_MID]
    base = HALF + NS_MID
    plain[base : base + NS_LOW, 0:NS_LOW] = matrices[0, 0:NS_LOW, 0:NS_LOW]
    high, low = halves(plain[...])
    target[:, 0:HALF] = high
    target[:, HALF : 2 * HALF] = high
    target[:, 2 * HALF :] = low


def react_kernel(
    block_x, block_y, comp, cell, level, table, rate, implicit, out, means,
    left, left_rim, mixed, plain, left_rate, left_implicit,
):
    species = comp.shape[0]
    span_x = block_x + 2 * R
    piece = 2048

    @pl.when(pl.program_id(0) == 0)
    def _():
        mixed[...] = jnp.zeros_like(mixed)
        stack_levels(left_rate, plain, rate)
        stack_levels(left_implicit, plain, implicit)
        high, low = halves(table[0:span_x].reshape(span_x * ROWS, block_y))
        left[:, 0:block_y] = high
        left[:, block_y:] = low
        value = table[span_x]
        high = value.astype(BF).astype(F32)
        lane = lax.broadcasted_iota(jnp.int32, value.shape, 1)
        low = roll(value - high, HALF)
        left_rim[...] = jnp.where(lane < HALF, high, low).astype(BF)
        for x in range(block_x):
            means[:, x, :] = table[x + R, 0:species, :]

    def choose(test, yes, no):
        shape = (yes.shape[0] // 8, 8, piece)
        return jnp.where(test[None], yes.reshape(shape), no.reshape(shape)).reshape(yes.shape)

    def work(at):
        span = slice(at, at + piece)
        local_x, inner, rim = positions(cell[:, span], block_x, block_y)
        hot = one_hot(inner, block_y)
        hot_rim = one_hot(rim, HALF)
        rows = jnp.dot(left[...], jnp.concatenate([hot, hot], 0), preferred_element_type=F32)
        on_rim = jnp.dot(
            left_rim[...], jnp.concatenate([hot_rim, hot_rim], 0), preferred_element_type=F32
        )
        place = jnp.broadcast_to(local_x, (8, piece))
        parts = [rows[x * ROWS : (x + 1) * ROWS] for x in range(span_x)]
        bit = 1
        while len(parts) > 1:
            test = (place & bit) != 0
            paired = [
                choose(test, parts[i + 1], parts[i]) for i in range(0, len(parts) - 1, 2)
            ]
            parts = paired + parts[2 * len(paired) :]
            bit *= 2
        taken = choose(jnp.broadcast_to(inner, (8, piece)) < 0, on_rim, parts[0])
        factor = taken[species + 1 : species + 2]
        comp_value = comp[:, span]
        mixed[0:species, span] = comp_value - factor * (comp_value - taken[0:species])
        levels = jnp.broadcast_to(level[:, span], (8, piece))
        full, middle = levels == 2, levels == 1
        base = HALF + NS_MID

        def pick(value):
            return choose(
                full, value[0:NS_MID],
                choose(middle, value[HALF:base], value[base : base + NS_MID]),
            )

        high, low = halves(mixed[:, span])
        right = jnp.concatenate([high, low, high], 0)
        drive = jnp.dot(left_rate[...], right, preferred_element_type=F32)
        source = jnp.tanh(jnp.concatenate([pick(drive), drive[NS_MID:HALF]], 0))
        high, low = halves(source)
        right = jnp.concatenate([high, low, high], 0)
        change = jnp.dot(left_implicit[...], right, preferred_element_type=F32)
        rest = change[NS_MID:ROWS]
        rest = choose(full, rest, jnp.zeros_like(rest))
        out[0:NS_MID, span] = mixed[0:NS_MID, span] + chem_step * pick(change)
        out[NS_MID:, span] = mixed[NS_MID:species, span] + chem_step * rest[0 : species - NS_MID]

    for at in range(0, comp.shape[1], piece):
        work(at)


def per_device(
    counts, composition, particle_mass, particle_cell, particle_level,
    les_mean, mix_rate, rate_matrix, implicit_map,
):
    species, particles = composition.shape
    block_x, block_y = les_mean.shape[1], les_mean.shape[2]
    span_x = block_x + 2 * R
    whole = pl.BlockSpec(memory_space=pltpu.VMEM)
    chunk = 4096
    steps = particles // chunk
    left_rows = span_x // 4 * 2 * ROWS

    def first_pass(rows):
        return pl.BlockSpec((rows, chunk), lambda i: (0, jnp.minimum(i, steps - 1)))

    dma = pltpu.SemaphoreType.DMA
    tiles = (span_x + 1, ROWS, LANES)
    table = pl.pallas_call(
        functools.partial(sums_kernel, counts, steps, chunk, block_x, block_y),
        grid=(2 * steps,),
        out_shape=jax.ShapeDtypeStruct(tiles, F32),
        in_specs=[
            first_pass(species),
            first_pass(1),
            pl.BlockSpec((2, chunk), lambda i: (0, i % steps)),
            pl.BlockSpec(les_mean.shape, lambda i: (0, 0, 0)),
            pl.BlockSpec(mix_rate.shape, lambda i: (0, 0)),
        ],
        out_specs=pl.BlockSpec(tiles, lambda i: (0, 0, 0)),
        scratch_shapes=[
            pltpu.VMEM((steps, 2 * block_y, chunk), BF),
            pltpu.VMEM((HALF, chunk), BF),
            pltpu.VMEM((ROWS, chunk), F32),
            pltpu.VMEM((steps, 2 * ROWS, chunk), BF),
            pltpu.VMEM((left_rows, 2 * block_y), F32),
            pltpu.VMEM((2 * ROWS, LANES), F32),
            pltpu.VMEM(tiles, F32),
            pltpu.VMEM((block_x, ROWS, block_y), F32),
            pltpu.VMEM((2, W + 1, ROWS, LANES), F32),
            pltpu.VMEM((2, ROWS, LANES), F32),
            pltpu.VMEM((2, 2, ROWS, LANES), F32),
            dma((2,)), dma((2,)), dma((8,)), dma((8,)),
        ],
        compiler_params=pltpu.CompilerParams(
            collective_id=0, has_side_effects=True, vmem_limit_bytes=60 << 20
        ),
    )(composition, particle_mass[None], particle_cell, les_mean, mix_rate)
    stacked = HALF + 2 * NS_MID
    chunk = 2048

    def by_chunk(rows):
        return pl.BlockSpec((rows, chunk), lambda i: (0, i))

    def fixed(array):
        return pl.BlockSpec(array.shape, lambda i: (0,) * array.ndim)

    return pl.pallas_call(
        functools.partial(react_kernel, block_x, block_y),
        grid=(particles // chunk,),
        out_shape=(
            jax.ShapeDtypeStruct(composition.shape, F32),
            jax.ShapeDtypeStruct(les_mean.shape, F32),
        ),
        in_specs=[
            by_chunk(species), by_chunk(2), by_chunk(1),
            fixed(table), fixed(rate_matrix), fixed(implicit_map),
        ],
        out_specs=(by_chunk(species), fixed(les_mean)),
        scratch_shapes=[
            pltpu.VMEM((span_x * ROWS, 2 * block_y), BF),
            pltpu.VMEM((ROWS, LANES), BF),
            pltpu.VMEM((HALF, chunk), F32),
            pltpu.VMEM((stacked, HALF), F32),
            pltpu.VMEM((stacked, 3 * HALF), BF),
            pltpu.VMEM((stacked, 3 * HALF), BF),
        ],
        compiler_params=pltpu.CompilerParams(vmem_limit_bytes=40 << 20),
    )(composition, particle_cell, particle_level[None], table, rate_matrix, implicit_map)


def solution(mesh):
    placed = (
        P(None, ("gx", "gy")),
        P(("gx", "gy")),
        P(None, ("gx", "gy")),
        P(("gx", "gy")),
        P(None, "gx", "gy"),
        P("gx", "gy"),
        P(),
        P(),
    )
    return jax.shard_map(
        functools.partial(per_device, (mesh.shape["gx"], mesh.shape["gy"])),
        mesh=mesh,
        in_specs=placed,
        out_specs=(P(None, ("gx", "gy")), P(None, "gx", "gy")),
        check_vma=False,
    )
```

profile of v0, /device:TPU:17, one launch (start us, length us, event | category | flops | bytes accessed | tf_op | source)
XLA Modules:
  0.0 20.1 jit_solution(6673592032829468436)
XLA Ops:
  0.6 0.0 copy-start.2
  0.6 0.0 copy-start
  0.7 0.0 copy-start.4
  0.7 0.0 copy-start.3
  0.7 0.0 copy-start.5
  0.7 12.1 %shard_map.95.table = f32[9,56,128]{2,1,0:T(8,128)} custom-call(f32[53,8192]{1,0:T(8,128)} %comp.3, f32[1,8192]{1,0:T(1,128)} %bitcast.3, s32[2,8192]{1,0:T(2,128)} %cell.3, f32[53,4,128]{2,1,0:T(4,128)} %les.1, f32[4,128]{1,0:T(4,128)} %rate.2), custom_call_target="tpu_custom_call" | custom-call | tf_op jit(solution)/shard_map/pallas_call | solution.py:404
  12.8 0.0 copy-done.2
  12.8 0.0 copy-done
  12.8 0.0 copy-done.4
  12.8 0.0 copy-done.3
  12.8 0.0 copy-done.5
  12.8 0.0 copy-start.1
  12.9 0.9 %copy-done.1 = f32[9,56,128]{2,1,0:T(8,128)S(1)} copy-done((f32[9,56,128]{2,1,0:T(8,128)S(1)}, f32[9,56,128]{2,1,0:T(8,128)}, u32[]{:S(2)}) %copy-start.1) | copy-done | bytes 258072
  13.8 6.3 %shard_map.96 = (f32[53,8192]{1,0:T(8,128)}, f32[53,4,128]{2,1,0:T(4,128)}) custom-call(f32[53,8192]{1,0:T(8,128)S(1)} %copy-done, s32[2,8192]{1,0:T(2,128)S(1)} %copy-done.2, s32[1,8192]{1,0:T(1,128)S(1)} %bitcast.2, f32[9,56,128]{2,1,0:T(8,128)S(1)} %copy-done.1, f32[3,53,53]{2,1,0:T(8,128)S(1)} %copy-done.3, f32[3,53,53]{2,1,0:T(8,128)S(1)} %copy-done.4), custom_call_target="tpu_custom_call" | custom-call | tf_op jit(solution)/shard_map/pallas_call | solution.py:443
Async XLA Ops:
  0.6 12.2 %copy-start.2 = (s32[2,8192]{1,0:T(2,128)S(1)}, s32[2,8192]{1,0:T(2,128)}, u32[]{:S(2)}) copy-start(s32[2,8192]{1,0:T(2,128)} %cell.3) | copy-start | bytes 196612
  0.6 12.2 %copy-start = (f32[53,8192]{1,0:T(8,128)S(1)}, f32[53,8192]{1,0:T(8,128)}, u32[]{:S(2)}) copy-start(f32[53,8192]{1,0:T(8,128)} %comp.3) | copy-start | bytes 5210116
  0.7 12.2 %copy-start.4 = (f32[3,53,53]{2,1,0:T(8,128)S(1)}, f32[3,53,53]{2,1,0:T(8,128)}, u32[]{:S(2)}) copy-start(f32[3,53,53]{2,1,0:T(8,128)} %implicit.1) | copy-start | bytes 101128
  0.7 12.2 %copy-start.3 = (f32[3,53,53]{2,1,0:T(8,128)S(1)}, f32[3,53,53]{2,1,0:T(8,128)}, u32[]{:S(2)}) copy-start(f32[3,53,53]{2,1,0:T(8,128)} %rate.3) | copy-start | bytes 101128
  0.7 12.2 %copy-start.5 = (s32[8192]{0:T(1024)S(1)}, s32[8192]{0:T(1024)}, u32[]{:S(2)}) copy-start(s32[8192]{0:T(1024)} %param.11) | copy-start | bytes 98308
  12.8 0.9 %copy-start.1 = (f32[9,56,128]{2,1,0:T(8,128)S(1)}, f32[9,56,128]{2,1,0:T(8,128)}, u32[]{:S(2)}) copy-start(f32[9,56,128]{2,1,0:T(8,128)} %shard_map.95.table) | copy-start | bytes 774148
where the time goes:
time: 20.2 us; the launch traced here: 20.1 us
  Pallas kernels  18.4 us (91%)
  local copies, waits for them, and re-layouts  0.96 us (5%)
  between operations  0.73 us (4%)
    pallas_call x1, Pallas kernels, per_device(): pl.pallas_call(functools.partial(sums_kernel, counts, steps, chunk, block...  12.1 us
    pallas_call x1, Pallas kernels, per_device(): pl.pallas_call(functools.partial(react_kernel, block_x, block_y), grid=(p...  6.28 us
    unnamed x12, local copies, waits for them, and re-layouts  0.96 us

commit v1 on v0

--- a/solution.py
+++ b/solution.py
@@ -404,7 +404,7 @@
     table = pl.pallas_call(
         functools.partial(sums_kernel, counts, steps, chunk, block_x, block_y),
         grid=(2 * steps,),
-        out_shape=jax.ShapeDtypeStruct(tiles, F32),
+        out_shape=pltpu.VMEM(tiles, F32),
         in_specs=[
             first_pass(species),
             first_pass(1),
@@ -412,7 +412,7 @@
             pl.BlockSpec(les_mean.shape, lambda i: (0, 0, 0)),
             pl.BlockSpec(mix_rate.shape, lambda i: (0, 0)),
         ],
-        out_specs=pl.BlockSpec(tiles, lambda i: (0, 0, 0)),
+        out_specs=pl.BlockSpec(memory_space=pltpu.VMEM),
         scratch_shapes=[
             pltpu.VMEM((steps, 2 * block_y, chunk), BF),
             pltpu.VMEM((HALF, chunk), BF),

time: 20.2 us -> 18.6 us (0.921)
  the two profiles are of different devices: /device:TPU:17 before, /device:TPU:19 now
where the time goes in v1:
time: 18.6 us; the launch traced here: 18.5 us
  Pallas kernels  17.7 us (95%)
  between operations  0.72 us (4%)
    pallas_call x1, Pallas kernels, per_device(): pl.pallas_call(functools.partial(sums_kernel, counts, steps, chunk, block...  11.5 us
    pallas_call x1, Pallas kernels, per_device(): pl.pallas_call(functools.partial(react_kernel, block_x, block_y), grid=(p...  6.29 us

profile of v1, /device:TPU:19, one launch (start us, length us, event | category | flops | bytes accessed | tf_op | source)
XLA Modules:
  0.0 18.5 jit_solution(4690246919448619144)
XLA Ops:
  0.6 0.0 copy-start.1
  0.6 0.0 copy-start
  0.7 0.0 copy-start.3
  0.7 0.0 copy-start.2
  0.7 0.0 copy-start.4
  0.7 11.5 %shard_map.95.table = f32[9,56,128]{2,1,0:T(8,128)S(1)} custom-call(f32[53,8192]{1,0:T(8,128)} %comp.3, f32[1,8192]{1,0:T(1,128)} %bitcast.3, s32[2,8192]{1,0:T(2,128)} %cell.3, f32[53,4,128]{2,1,0:T(4,128)} %les.1, f32[4,128]{1,0:T(4,128)} %rate.2), custom_call_target="tpu_custom_call" | custom-call | tf_op jit(solution)/shard_map/pallas_call | solution.py:404
  12.1 0.0 copy-done.1
  12.2 0.0 copy-done
  12.2 0.0 copy-done.3
  12.2 0.0 copy-done.2
  12.2 0.0 copy-done.4
  12.2 6.3 %shard_map.96 = (f32[53,8192]{1,0:T(8,128)}, f32[53,4,128]{2,1,0:T(4,128)}) custom-call(f32[53,8192]{1,0:T(8,128)S(1)} %copy-done, s32[2,8192]{1,0:T(2,128)S(1)} %copy-done.1, s32[1,8192]{1,0:T(1,128)S(1)} %bitcast.2, f32[9,56,128]{2,1,0:T(8,128)S(1)} %shard_map.95.table, f32[3,53,53]{2,1,0:T(8,128)S(1)} %copy-done.2, f32[3,53,53]{2,1,0:T(8,128)S(1)} %copy-done.3), custom_call_target="tpu_custom_call" | custom-call | tf_op jit(solution)/shard_map/pallas_call | solution.py:443
Async XLA Ops:
  0.6 11.5 %copy-start.1 = (s32[2,8192]{1,0:T(2,128)S(1)}, s32[2,8192]{1,0:T(2,128)}, u32[]{:S(2)}) copy-start(s32[2,8192]{1,0:T(2,128)} %cell.3) | copy-start | bytes 196612
  0.6 11.5 %copy-start = (f32[53,8192]{1,0:T(8,128)S(1)}, f32[53,8192]{1,0:T(8,128)}, u32[]{:S(2)}) copy-start(f32[53,8192]{1,0:T(8,128)} %comp.3) | copy-start | bytes 5210116
  0.7 11.5 %copy-start.3 = (f32[3,53,53]{2,1,0:T(8,128)S(1)}, f32[3,53,53]{2,1,0:T(8,128)}, u32[]{:S(2)}) copy-start(f32[3,53,53]{2,1,0:T(8,128)} %implicit.1) | copy-start | bytes 101128
  0.7 11.5 %copy-start.2 = (f32[3,53,53]{2,1,0:T(8,128)S(1)}, f32[3,53,53]{2,1,0:T(8,128)}, u32[]{:S(2)}) copy-start(f32[3,53,53]{2,1,0:T(8,128)} %rate.3) | copy-start | bytes 101128
  0.7 11.5 %copy-start.4 = (s32[8192]{0:T(1024)S(1)}, s32[8192]{0:T(1024)}, u32[]{:S(2)}) copy-start(s32[8192]{0:T(1024)} %param.11) | copy-start | bytes 98308

commit v2 on v1

--- a/solution.py
+++ b/solution.py
@@ -294,58 +294,69 @@
                 main_copy(dx).wait_send()
 
 
-def stack_levels(target, plain, matrices):
+def stack_levels(plain, matrices):
     species = matrices.shape[1]
     plain[...] = jnp.zeros_like(plain)
     plain[0:species, 0:species] = matrices[2]
-    plain[HALF : HALF + NS_MID, 0:NS_MID] = matrices[1, 0:NS_MID, 0:NS_MID]
-    base = HALF + NS_MID
-    plain[base : base + NS_LOW, 0:NS_LOW] = matrices[0, 0:NS_LOW, 0:NS_LOW]
+    plain[0:NS_MID, ROWS : ROWS + NS_MID] = matrices[1, 0:NS_MID, 0:NS_MID]
+    plain[ROWS : ROWS + NS_LOW, ROWS : ROWS + NS_LOW] = matrices[0, 0:NS_LOW, 0:NS_LOW]
     high, low = halves(plain[...])
-    target[:, 0:HALF] = high
-    target[:, HALF : 2 * HALF] = high
-    target[:, 2 * HALF :] = low
+    return jnp.concatenate([high, high, low], 1)
 
 
 def react_kernel(
-    block_x, block_y, comp, cell, level, table, rate, implicit, out, means,
-    left, left_rim, mixed, plain, left_rate, left_implicit,
+    block_x, block_y, piece, group, comp, cell, level, table, rate, implicit, out, means,
+    left, left_rim, mixed, result, plain_rate, plain_implicit, done, done_means, staged,
+    source, left_rate, left_implicit,
 ):
     species = comp.shape[0]
+    particles = comp.shape[1]
     span_x = block_x + 2 * R
-    piece = 2048
-
-    @pl.when(pl.program_id(0) == 0)
-    def _():
-        mixed[...] = jnp.zeros_like(mixed)
-        stack_levels(left_rate, plain, rate)
-        stack_levels(left_implicit, plain, implicit)
-        high, low = halves(table[0:span_x].reshape(span_x * ROWS, block_y))
-        left[:, 0:block_y] = high
-        left[:, block_y:] = low
-        value = table[span_x]
-        high = value.astype(BF).astype(F32)
-        lane = lax.broadcasted_iota(jnp.int32, value.shape, 1)
-        low = roll(value - high, HALF)
-        left_rim[...] = jnp.where(lane < HALF, high, low).astype(BF)
-        for x in range(block_x):
-            means[:, x, :] = table[x + R, 0:species, :]
+    pairs = span_x // 2
+    for parity in range(2):
+        value = jnp.concatenate([table[2 * g + parity] for g in range(pairs)], 0)
+        high, low = halves(value)
+        left[:, parity * block_y : (parity + 1) * block_y] = high
+        left[:, (2 + parity) * block_y : (3 + parity) * block_y] = low
+    value = table[span_x]
+    high = value.astype(BF).astype(F32)
+    lane = lax.broadcasted_iota(jnp.int32, value.shape, 1)
+    low = roll(value - high, HALF)
+    left_rim[...] = jnp.where(lane < HALF, high, low).astype(BF)
+    mixed[species:, :] = jnp.zeros((ROWS - species, particles), F32)
+    left_rate[...] = stack_levels(plain_rate, rate)
+    left_implicit[...] = stack_levels(plain_implicit, implicit)
 
     def choose(test, yes, no):
         shape = (yes.shape[0] // 8, 8, piece)
         return jnp.where(test[None], yes.reshape(shape), no.reshape(shape)).reshape(yes.shape)
 
-    def work(at):
-        span = slice(at, at + piece)
+    def act(matrix, value, full, middle):
+        zero = jnp.zeros_like(value)
+        slots = jnp.concatenate(
+            [choose(full, value, zero), choose(full, zero[0:NS_MID], value[0:NS_MID])], 0
+        )
+        high, low = halves(slots)
+        right = jnp.concatenate([high, low, high], 0)
+        got = jnp.dot(matrix, right, preferred_element_type=F32)
+        first = choose(middle, got[ROWS:], got[0:NS_MID])
+        return jnp.concatenate([first, got[NS_MID:ROWS]], 0)
+
+    def copy(k):
+        span = pl.ds(k * group, group)
+        return pltpu.make_async_copy(result.at[:, span], out.at[:, span], done.at[k])
+
+    def gather(span):
         local_x, inner, rim = positions(cell[:, span], block_x, block_y)
-        hot = one_hot(inner, block_y)
+        column = jnp.where(inner < 0, -1, inner + (local_x % 2) * block_y)
+        hot = one_hot(column, 2 * block_y)
         hot_rim = one_hot(rim, HALF)
         rows = jnp.dot(left[...], jnp.concatenate([hot, hot], 0), preferred_element_type=F32)
         on_rim = jnp.dot(
             left_rim[...], jnp.concatenate([hot_rim, hot_rim], 0), preferred_element_type=F32
         )
-        place = jnp.broadcast_to(local_x, (8, piece))
-        parts = [rows[x * ROWS : (x + 1) * ROWS] for x in range(span_x)]
+        place = jnp.broadcast_to(local_x // 2, (8, piece))
+        parts = [rows[g * ROWS : (g + 1) * ROWS] for g in range(pairs)]
         bit = 1
         while len(parts) > 1:
             test = (place & bit) != 0
@@ -358,30 +369,38 @@
         factor = taken[species + 1 : species + 2]
         comp_value = comp[:, span]
         mixed[0:species, span] = comp_value - factor * (comp_value - taken[0:species])
+
+    def tests(span):
         levels = jnp.broadcast_to(level[:, span], (8, piece))
-        full, middle = levels == 2, levels == 1
-        base = HALF + NS_MID
-
-        def pick(value):
-            return choose(
-                full, value[0:NS_MID],
-                choose(middle, value[HALF:base], value[base : base + NS_MID]),
-            )
-
-        high, low = halves(mixed[:, span])
-        right = jnp.concatenate([high, low, high], 0)
-        drive = jnp.dot(left_rate[...], right, preferred_element_type=F32)
-        source = jnp.tanh(jnp.concatenate([pick(drive), drive[NS_MID:HALF]], 0))
-        high, low = halves(source)
-        right = jnp.concatenate([high, low, high], 0)
-        change = jnp.dot(left_implicit[...], right, preferred_element_type=F32)
-        rest = change[NS_MID:ROWS]
-        rest = choose(full, rest, jnp.zeros_like(rest))
-        out[0:NS_MID, span] = mixed[0:NS_MID, span] + chem_step * pick(change)
-        out[NS_MID:, span] = mixed[NS_MID:species, span] + chem_step * rest[0 : species - NS_MID]
-
-    for at in range(0, comp.shape[1], piece):
-        work(at)
+        return levels == 2, levels == 0
+
+    def drive(span):
+        source[:, span] = jnp.tanh(act(left_rate[...], mixed[:, span], *tests(span)))
+
+    def finish(span):
+        change = act(left_implicit[...], source[:, span], *tests(span))
+        updated = mixed[:, span] + chem_step * change
+        result[:, span] = updated[0:species]
+
+    count = particles // piece
+    spans = [slice(k * piece, (k + 1) * piece) for k in range(count)]
+    for k in range(count + 2):
+        if k < count:
+            gather(spans[k])
+        if 0 <= k - 1 < count:
+            drive(spans[k - 1])
+        if 0 <= k - 2:
+            finish(spans[k - 2])
+            if (k - 1) * piece % group == 0:
+                copy((k - 1) * piece // group - 1).start()
+        if k == 1:
+            for x in range(block_x):
+                staged[:, x, :] = table[x + R, 0:species, :]
+            send_means = pltpu.make_async_copy(staged, means, done_means)
+            send_means.start()
+    send_means.wait()
+    for k in range(particles // group):
+        copy(k).wait()
 
 
 def per_device(
@@ -431,34 +450,29 @@
             collective_id=0, has_side_effects=True, vmem_limit_bytes=60 << 20
         ),
     )(composition, particle_mass[None], particle_cell, les_mean, mix_rate)
-    stacked = HALF + 2 * NS_MID
-    chunk = 2048
-
-    def by_chunk(rows):
-        return pl.BlockSpec((rows, chunk), lambda i: (0, i))
-
-    def fixed(array):
-        return pl.BlockSpec(array.shape, lambda i: (0,) * array.ndim)
-
+    piece = 512
+    group = 2048
     return pl.pallas_call(
-        functools.partial(react_kernel, block_x, block_y),
-        grid=(particles // chunk,),
+        functools.partial(react_kernel, block_x, block_y, piece, group),
         out_shape=(
             jax.ShapeDtypeStruct(composition.shape, F32),
             jax.ShapeDtypeStruct(les_mean.shape, F32),
         ),
-        in_specs=[
-            by_chunk(species), by_chunk(2), by_chunk(1),
-            fixed(table), fixed(rate_matrix), fixed(implicit_map),
-        ],
-        out_specs=(by_chunk(species), fixed(les_mean)),
+        in_specs=[whole] * 6,
+        out_specs=[pl.BlockSpec(memory_space=pl.ANY)] * 2,
         scratch_shapes=[
-            pltpu.VMEM((span_x * ROWS, 2 * block_y), BF),
+            pltpu.VMEM((span_x // 2 * ROWS, 4 * block_y), BF),
             pltpu.VMEM((ROWS, LANES), BF),
-            pltpu.VMEM((HALF, chunk), F32),
-            pltpu.VMEM((stacked, HALF), F32),
-            pltpu.VMEM((stacked, 3 * HALF), BF),
-            pltpu.VMEM((stacked, 3 * HALF), BF),
+            pltpu.VMEM((ROWS, particles), F32),
+            pltpu.VMEM(composition.shape, F32),
+            pltpu.VMEM((ROWS + NS_MID, ROWS + NS_MID), F32),
+            pltpu.VMEM((ROWS + NS_MID, ROWS + NS_MID), F32),
+            dma((particles // group,)),
+            dma(()),
+            pltpu.VMEM(les_mean.shape, F32),
+            pltpu.VMEM((ROWS, particles), F32),
+            pltpu.VMEM((ROWS + NS_MID, 3 * (ROWS + NS_MID)), BF),
+            pltpu.VMEM((ROWS + NS_MID, 3 * (ROWS + NS_MID)), BF),
         ],
         compiler_params=pltpu.CompilerParams(vmem_limit_bytes=40 << 20),
     )(composition, particle_cell, particle_level[None], table, rate_matrix, implicit_map)

time: 18.6 us -> 17.9 us (0.962)
  Pallas kernels: 17.7 us -> 17.1 us
    pallas_call x1, Pallas kernels: 6.29 us -> 5.6 us  [per_device(): pl.pallas_call(functools.partial(react_kernel, block_x, block_y, piece, g...]
where the time goes in v2:
time: 17.9 us; the launch traced here: 17.8 us
  Pallas kernels  17.1 us (96%)
  between operations  0.72 us (4%)
    pallas_call x1, Pallas kernels, per_device(): pl.pallas_call(functools.partial(sums_kernel, counts, steps, chunk, block...  11.5 us
    pallas_call x1, Pallas kernels, per_device(): pl.pallas_call(functools.partial(react_kernel, block_x, block_y, piece, g...  5.6 us

profile of v2, /device:TPU:19, one launch (start us, length us, event | category | flops | bytes accessed | tf_op | source)
XLA Modules:
  0.0 17.8 jit_solution(4442278235838804895)
XLA Ops:
  0.6 0.0 copy-start.1
  0.6 0.0 copy-start
  0.7 0.0 copy-start.3
  0.7 0.0 copy-start.2
  0.7 0.0 copy-start.4
  0.7 11.5 %shard_map.95.table = f32[9,56,128]{2,1,0:T(8,128)S(1)} custom-call(f32[53,8192]{1,0:T(8,128)} %comp.3, f32[1,8192]{1,0:T(1,128)} %bitcast.3, s32[2,8192]{1,0:T(2,128)} %cell.3, f32[53,4,128]{2,1,0:T(4,128)} %les.1, f32[4,128]{1,0:T(4,128)} %rate.2), custom_call_target="tpu_custom_call" | custom-call | tf_op jit(solution)/shard_map/pallas_call | solution.py:423
  12.1 0.0 copy-done.1
  12.2 0.0 copy-done
  12.2 0.0 copy-done.3
  12.2 0.0 copy-done.2
  12.2 0.0 copy-done.4
  12.2 5.6 %shard_map.96 = (f32[53,8192]{1,0:T(8,128)}, f32[53,4,128]{2,1,0:T(4,128)}) custom-call(f32[53,8192]{1,0:T(8,128)S(1)} %copy-done, s32[2,8192]{1,0:T(2,128)S(1)} %copy-done.1, s32[1,8192]{1,0:T(1,128)S(1)} %bitcast.2, f32[9,56,128]{2,1,0:T(8,128)S(1)} %shard_map.95.table, f32[3,53,53]{2,1,0:T(8,128)S(1)} %copy-done.2, f32[3,53,53]{2,1,0:T(8,128)S(1)} %copy-done.3), custom_call_target="tpu_custom_call" | custom-call | tf_op jit(solution)/shard_map/pallas_call | solution.py:455
Async XLA Ops:
  0.6 11.5 %copy-start.1 = (s32[2,8192]{1,0:T(2,128)S(1)}, s32[2,8192]{1,0:T(2,128)}, u32[]{:S(2)}) copy-start(s32[2,8192]{1,0:T(2,128)} %cell.3) | copy-start | bytes 196612
  0.6 11.5 %copy-start = (f32[53,8192]{1,0:T(8,128)S(1)}, f32[53,8192]{1,0:T(8,128)}, u32[]{:S(2)}) copy-start(f32[53,8192]{1,0:T(8,128)} %comp.3) | copy-start | bytes 5210116
  0.7 11.5 %copy-start.3 = (f32[3,53,53]{2,1,0:T(8,128)S(1)}, f32[3,53,53]{2,1,0:T(8,128)}, u32[]{:S(2)}) copy-start(f32[3,53,53]{2,1,0:T(8,128)} %implicit.1) | copy-start | bytes 101128
  0.7 11.5 %copy-start.2 = (f32[3,53,53]{2,1,0:T(8,128)S(1)}, f32[3,53,53]{2,1,0:T(8,128)}, u32[]{:S(2)}) copy-start(f32[3,53,53]{2,1,0:T(8,128)} %rate.3) | copy-start | bytes 101128
  0.7 11.5 %copy-start.4 = (s32[8192]{0:T(1024)S(1)}, s32[8192]{0:T(1024)}, u32[]{:S(2)}) copy-start(s32[8192]{0:T(1024)} %param.11) | copy-start | bytes 98308

commit v3 on v2

v3 whole, which is shorter than its diff:
```python
import functools

import jax
import jax.numpy as jnp
from jax import lax
from jax.experimental import pallas as pl
from jax.experimental.pallas import tpu as pltpu
from jax.sharding import PartitionSpec as P

NS_LOW = 21
NS_MID = 24
R = 2
W = 2 * R
HALF = 64
ROWS = 56
LANES = 128

prior_weight = 16.0
chem_step = 0.5
BF = jnp.bfloat16
F32 = jnp.float32
MESH = pl.DeviceIdType.MESH


def halves(value):
    high = value.astype(BF)
    return high, (value - high.astype(F32)).astype(BF)


def roll(value, shift):
    return pltpu.roll(value, shift % value.shape[1], 1)


def positions(cell, block_x, block_y):
    local_x = cell[0:1] - (lax.axis_index("gx") * block_x - R)
    local_y = cell[1:2] - (lax.axis_index("gy") * block_y - R)
    low_rim = local_y < W
    on_rim = low_rim | (local_y >= block_y)
    rim = jnp.where(low_rim, local_y, local_y - block_y + (block_x + 2 * R) * W) + local_x * W
    return local_x, on_rim, rim, local_y - R


def one_hot(place, rows):
    sub = lax.broadcasted_iota(jnp.int32, (rows, place.shape[1]), 0)
    same = sub.astype(F32).astype(BF) == jnp.broadcast_to(
        place.astype(F32), (rows, place.shape[1])
    ).astype(BF)
    return jnp.where(same, jnp.ones((), BF), jnp.zeros((), BF))


def prior_of(x, species, les, rate):
    mass = jnp.full((1, LANES), prior_weight, F32)
    fade = 1.0 - jnp.exp(-rate[x : x + 1, :])
    rest = jnp.zeros((ROWS - species - 2, LANES), F32)
    return jnp.concatenate([prior_weight * les[:, x, :], mass, fade, rest], 0)


def sums_kernel(
    counts, chunk, block_x, block_y, comp, mass, cell_in, les_in, rate_in, table,
    data, weight, weighted, cell, les, rate, hot, both, codes, acc, send, prior, plain, from_x, from_y, from_xy,
    comp_sem, small_sem, send_main, recv_main, send_rim, recv_rim,
):
    species, particles = comp.shape
    span_x = block_x + 2 * R
    pairs = span_x // 2
    side_size = span_x * W
    tall = 2 * ROWS
    chunks = particles // chunk
    gx, gy = lax.axis_index("gx"), lax.axis_index("gy")
    upper_first = gx % 2
    has = {
        -1: (gx > 0, gy > 0),
        1: (gx < counts[0] - 1, gy < counts[1] - 1),
        0: (True, True),
    }
    others = [(dx, dy) for dx in (-1, 0, 1) for dy in (-1, 0, 1) if (dx, dy) != (0, 0)]
    lane = lax.broadcasted_iota(jnp.int32, (ROWS, LANES), 1)
    row = lax.broadcasted_iota(jnp.int32, (ROWS, LANES), 0)
    inside = (lane >= R) & (lane < block_y - R)

    def chunk_copy(k):
        span = pl.ds(k * chunk, chunk)
        return pltpu.make_async_copy(
            comp.at[:, span], data.at[:, span], comp_sem.at[k]
        )

    small = [
        pltpu.make_async_copy(cell_in, cell, small_sem.at[0]),
        pltpu.make_async_copy(mass, weight, small_sem.at[1]),
        pltpu.make_async_copy(les_in, les, small_sem.at[2]),
        pltpu.make_async_copy(rate_in, rate, small_sem.at[3]),
    ]
    small[0].start()
    small[1].start()
    for k in range(chunks):
        chunk_copy(k).start()
    small[2].start()
    small[3].start()

    def present(dx, dy):
        return jnp.logical_and(has[dx][0], has[dy][1])

    def landing(dx, dy):
        if dy == 0:
            return from_x.at[(dx + 1) // 2, W]
        if dx == 0:
            return from_y.at[(dy + 1) // 2]
        return from_xy.at[(dx + 1) // 2, (dy + 1) // 2]

    def main_copy(dx):
        first = 0 if dx < 0 else block_x
        return pltpu.make_async_remote_copy(
            src_ref=send.at[pl.ds(first, W)],
            dst_ref=from_x.at[(1 - dx) // 2, pl.ds(0, W)],
            send_sem=send_main.at[(dx + 1) // 2],
            recv_sem=recv_main.at[(1 - dx) // 2],
            device_id=(gx + dx, gy),
            device_id_type=MESH,
        )

    def rim_copy(k, dx, dy):
        return pltpu.make_async_remote_copy(
            src_ref=send.at[span_x],
            dst_ref=landing(-dx, -dy),
            send_sem=send_rim.at[k],
            recv_sem=recv_rim.at[len(others) - 1 - k],
            device_id=(gx + dx, gy + dy),
            device_id_type=MESH,
        )

    def main_arrival(dx):
        return pltpu.make_async_remote_copy(
            src_ref=send.at[pl.ds(0, W)],
            dst_ref=from_x.at[(dx + 1) // 2, pl.ds(0, W)],
            send_sem=send_main.at[(dx + 1) // 2],
            recv_sem=recv_main.at[(dx + 1) // 2],
            device_id=(gx + dx, gy),
            device_id_type=MESH,
        )

    def rim_arrival(k, dx, dy):
        return pltpu.make_async_remote_copy(
            src_ref=send.at[span_x],
            dst_ref=landing(dx, dy),
            send_sem=send_rim.at[k],
            recv_sem=recv_rim.at[k],
            device_id=(gx + dx, gy + dy),
            device_id_type=MESH,
        )

    barrier = pltpu.get_barrier_semaphore()
    for dx, dy in others:
        @pl.when(present(dx, dy))
        def _():
            pl.semaphore_signal(
                barrier, inc=1, device_id=(gx + dx, gy + dy), device_id_type=MESH
            )
    weighted[species:, :] = jnp.zeros((ROWS - species, particles), F32)
    prior[...] = jnp.zeros_like(prior)
    for dx in (-1, 1):
        @pl.when(jnp.logical_not(has[dx][0]))
        def _():
            from_x[(dx + 1) // 2] = jnp.zeros((W + 1, ROWS, LANES), F32)
    for dx, dy in others:
        if dy != 0:
            @pl.when(jnp.logical_not(present(dx, dy)))
            def _():
                landing(dx, dy)[...] = jnp.zeros((ROWS, LANES), F32)

    def add_up(start, size, groups, first, fresh):
        for part in range(2):
            span = slice(start + part * (size // 2), start + (part + 1) * (size // 2))
            code = jnp.broadcast_to(codes[:, span], (16, size // 2)).astype(BF)
            value = both[:, span]
            rows = []
            for group in groups:
                keep = jnp.where(code == group, jnp.ones((), BF), jnp.zeros((), BF))
                rows.append(value * jnp.concatenate([keep] * (tall // 16), 0))
            got = lax.dot_general(
                jnp.concatenate(rows, 0), hot[:, span], (((1,), (1,)), ((), ())),
                preferred_element_type=F32,
            )
            if fresh:
                acc[part, first : first + len(groups) * tall] = got
            else:
                acc[part, first : first + len(groups) * tall] += got

    def total_of(at, cols):
        low, high = slice(at, at + ROWS), slice(at + ROWS, at + tall)
        return (acc[0, low, cols] + acc[1, low, cols]) + (acc[0, high, cols] + acc[1, high, cols])

    def half_tiles(base, first):
        for u in range(W):
            cols = slice((u % 2) * block_y, (u % 2 + 1) * block_y)
            t = first + u
            send[t] = total_of(base + (u // 2) * tall, cols) + prior[t]

    def prepare(k):
        for at in range(k * chunk, (k + 1) * chunk, 4 * LANES):
            span = slice(at, at + 4 * LANES)
            local_x, on_rim, rim, inner = positions(cell[:, span], block_x, block_y)
            hot[:, span] = one_hot(
                jnp.where(on_rim, rim, inner + (local_x % 2) * block_y), 2 * block_y
            )
            code = jnp.where(on_rim, pairs, (local_x // 2 + upper_first * (pairs // 2)) % pairs)
            codes[:, span] = code.astype(F32)
            weighted[0:species, span] = data[:, span] * weight[:, span]
            weighted[species : species + 1, span] = weight[:, span]
            value = weighted[:, span]
            high = value.astype(BF).astype(F32)
            both[:, span] = jnp.concatenate([high, value - high], 0).astype(BF)

    def set_prior():
        small[2].wait()
        small[3].wait()
        for x in range(block_x):
            own = prior_of(x, species, les, rate)
            plain[x] = own
            prior[x + R] = jnp.where(inside, own, 0.0)

    early = list(range(pairs // 2)) + [pairs]
    late = list(range(pairs // 2, pairs))
    small[0].wait()
    small[1].wait()
    late_at = len(early) * tall
    chunk_copy(0).wait()
    prepare(0)
    for k in range(chunks):
        @pl.when(gx >= 0)
        def _():
            if k + 1 < chunks:
                chunk_copy(k + 1).wait()
            add_up(k * chunk, chunk, early, 0, k == 0)
            if k + 1 < chunks:
                prepare(k + 1)
            else:
                set_prior()

    half_tiles(0, upper_first * block_x)
    rim_sum = total_of((pairs // 2) * tall, slice(0, LANES))
    for x in range(block_x):
        t = x + R
        low_at, high_at = t * W + R, side_size + t * W
        low, high = roll(plain[x], low_at), roll(plain[x], high_at + R)
        rim_sum += jnp.where((lane >= low_at) & (lane < low_at + R), low, 0.0)
        rim_sum += jnp.where((lane >= high_at) & (lane < high_at + R), high, 0.0)
    send[span_x] = rim_sum
    number = (1 + (gx > 0).astype(jnp.int32) + (gx < counts[0] - 1).astype(jnp.int32)) * (
        1 + (gy > 0).astype(jnp.int32) + (gy < counts[1] - 1).astype(jnp.int32)
    ) - 1
    pl.semaphore_wait(barrier, number)

    @pl.when(jnp.logical_and(upper_first == 0, has[-1][0]))
    def _():
        main_copy(-1).start()

    @pl.when(jnp.logical_and(upper_first == 1, has[1][0]))
    def _():
        main_copy(1).start()

    for k, (dx, dy) in enumerate(others):
        @pl.when(present(dx, dy))
        def _():
            rim_copy(k, dx, dy).start()

    @pl.when(gx >= 0)
    def _():
        add_up(0, particles, late, late_at, True)

    half_tiles(late_at, (1 - upper_first) * block_x)

    @pl.when(jnp.logical_and(upper_first == 1, has[-1][0]))
    def _():
        main_copy(-1).start()

    @pl.when(jnp.logical_and(upper_first == 0, has[1][0]))
    def _():
        main_copy(1).start()

    for k, (dx, dy) in enumerate(others):
        @pl.when(present(dx, dy))
        def _():
            rim_arrival(k, dx, dy).wait_recv()

    def finish(total):
        total_mass = total[species : species + 1, :]
        weight = jnp.where(total_mass > 0.0, total_mass, 1.0)
        weight = jnp.broadcast_to(weight, total.shape)
        return total / jnp.where(row < species, weight, 1.0)

    low_side = lane < side_size
    place_x = jnp.where(low_side, lane, lane - side_size)
    used = lane < 2 * side_size
    behind = used & (place_x < 2 * R * W)
    ahead = used & (place_x >= block_x * W)
    total = send[span_x]
    for dx, dy in others:
        mask = used if dx == 0 else behind if dx < 0 else ahead
        if dy != 0:
            mask = mask & (low_side if dy < 0 else jnp.logical_not(low_side))
        shift = dx * block_x * W + dy * side_size
        total = total + jnp.where(mask, roll(landing(dx, dy)[...], shift), 0.0)
    rim_value = finish(total)
    table[span_x] = rim_value

    def close(t):
        side, u = t // W, t % W
        value = finish(send[t] + from_x[side, u])
        if R <= t < R + block_x:
            low_at, high_at = t * W + R, side_size + t * W
            value = jnp.where(lane < R, roll(rim_value, -low_at), value)
            value = jnp.where(
                lane >= block_y - R, roll(rim_value, block_y - R - high_at), value
            )
        table[t] = value

    def close_half(dx):
        @pl.when(has[dx][0])
        def _():
            main_arrival(dx).wait_recv()

        first = 0 if dx < 0 else W
        for t in range(first, first + W):
            close(t)

    @pl.when(upper_first == 0)
    def _():
        close_half(-1)
        close_half(1)

    @pl.when(upper_first == 1)
    def _():
        close_half(1)
        close_half(-1)

    for k, (dx, dy) in enumerate(others):
        @pl.when(present(dx, dy))
        def _():
            rim_copy(k, dx, dy).wait_send()
    for dx in (-1, 1):
        @pl.when(has[dx][0])
        def _():
            main_copy(dx).wait_send()


def stack_levels(plain, matrices):
    species = matrices.shape[1]
    plain[...] = jnp.zeros_like(plain)
    plain[0:species, 0:species] = matrices[2]
    plain[0:NS_MID, ROWS : ROWS + NS_MID] = matrices[1, 0:NS_MID, 0:NS_MID]
    plain[ROWS : ROWS + NS_LOW, ROWS : ROWS + NS_LOW] = matrices[0, 0:NS_LOW, 0:NS_LOW]
    high, low = halves(plain[...])
    return jnp.concatenate([high, high, low], 1)


def react_kernel(
    block_x, block_y, piece, group, comp, cell, level, table, rate, implicit, out, means,
    left, left_rim, mixed, result, plain_rate, plain_implicit, done, done_means, staged,
    source, left_rate, left_implicit,
):
    species = comp.shape[0]
    particles = comp.shape[1]
    span_x = block_x + 2 * R
    pairs = span_x // 2
    for parity in range(2):
        value = jnp.concatenate([table[2 * g + parity] for g in range(pairs)], 0)
        high, low = halves(value)
        left[:, parity * block_y : (parity + 1) * block_y] = high
        left[:, (2 + parity) * block_y : (3 + parity) * block_y] = low
    value = table[span_x]
    high = value.astype(BF).astype(F32)
    lane = lax.broadcasted_iota(jnp.int32, value.shape, 1)
    low = roll(value - high, HALF)
    left_rim[...] = jnp.where(lane < HALF, high, low).astype(BF)
    mixed[species:, :] = jnp.zeros((ROWS - species, particles), F32)
    left_rate[...] = stack_levels(plain_rate, rate)
    left_implicit[...] = stack_levels(plain_implicit, implicit)

    def choose(test, yes, no):
        shape = (yes.shape[0] // 8, 8, piece)
        return jnp.where(test[None], yes.reshape(shape), no.reshape(shape)).reshape(yes.shape)

    def act(matrix, value, full, middle):
        zero = jnp.zeros_like(value)
        slots = jnp.concatenate(
            [choose(full, value, zero), choose(full, zero[0:NS_MID], value[0:NS_MID])], 0
        )
        high, low = halves(slots)
        right = jnp.concatenate([high, low, high], 0)
        got = jnp.dot(matrix, right, preferred_element_type=F32)
        first = choose(middle, got[ROWS:], got[0:NS_MID])
        return jnp.concatenate([first, got[NS_MID:ROWS]], 0)

    def copy(k):
        span = pl.ds(k * group, group)
        return pltpu.make_async_copy(result.at[:, span], out.at[:, span], done.at[k])

    def gather(span):
        local_x, on_rim, rim, inner = positions(cell[:, span], block_x, block_y)
        column = jnp.where(on_rim, -1, inner + (local_x % 2) * block_y)
        rim = jnp.where(on_rim, rim, -1)
        hot = one_hot(column, 2 * block_y)
        hot_rim = one_hot(rim, HALF)
        rows = jnp.dot(left[...], jnp.concatenate([hot, hot], 0), preferred_element_type=F32)
        rim_rows = jnp.dot(
            left_rim[...], jnp.concatenate([hot_rim, hot_rim], 0), preferred_element_type=F32
        )
        place = jnp.broadcast_to(local_x // 2, (8, piece))
        parts = [rows[g * ROWS : (g + 1) * ROWS] for g in range(pairs)]
        bit = 1
        while len(parts) > 1:
            test = (place & bit) != 0
            paired = [
                choose(test, parts[i + 1], parts[i]) for i in range(0, len(parts) - 1, 2)
            ]
            parts = paired + parts[2 * len(paired) :]
            bit *= 2
        taken = choose(jnp.broadcast_to(column, (8, piece)) < 0, rim_rows, parts[0])
        factor = taken[species + 1 : species + 2]
        comp_value = comp[:, span]
        mixed[0:species, span] = comp_value - factor * (comp_value - taken[0:species])

    def tests(span):
        levels = jnp.broadcast_to(level[:, span], (8, piece))
        return levels == 2, levels == 0

    def drive(span):
        source[:, span] = jnp.tanh(act(left_rate[...], mixed[:, span], *tests(span)))

    def finish(span):
        change = act(left_implicit[...], source[:, span], *tests(span))
        updated = mixed[:, span] + chem_step * change
        result[:, span] = updated[0:species]

    count = particles // piece
    spans = [slice(k * piece, (k + 1) * piece) for k in range(count)]
    for k in range(count + 2):
        if k < count:
            gather(spans[k])
        if 0 <= k - 1 < count:
            drive(spans[k - 1])
        if 0 <= k - 2:
            finish(spans[k - 2])
            if (k - 1) * piece % group == 0:
                copy((k - 1) * piece // group - 1).start()
        if k == 1:
            for x in range(block_x):
                staged[:, x, :] = table[x + R, 0:species, :]
            send_means = pltpu.make_async_copy(staged, means, done_means)
            send_means.start()
    send_means.wait()
    for k in range(particles // group):
        copy(k).wait()


def per_device(
    counts, composition, particle_mass, particle_cell, particle_level,
    les_mean, mix_rate, rate_matrix, implicit_map,
):
    species, particles = composition.shape
    block_x, block_y = les_mean.shape[1], les_mean.shape[2]
    span_x = block_x + 2 * R
    whole = pl.BlockSpec(memory_space=pltpu.VMEM)
    chunk = 2048
    hbm = pl.BlockSpec(memory_space=pltpu.HBM)
    inputs = composition, particle_mass[None], particle_cell, les_mean, mix_rate
    stay = [pltpu.with_memory_space_constraint(x, pltpu.HBM) for x in inputs]
    dma = pltpu.SemaphoreType.DMA
    tiles = (span_x + 1, ROWS, LANES)
    table = pl.pallas_call(
        functools.partial(sums_kernel, counts, chunk, block_x, block_y),
        out_shape=pltpu.VMEM(tiles, F32),
        in_specs=[hbm] * 5,
        out_specs=whole,
        scratch_shapes=[
            pltpu.VMEM(composition.shape, F32),
            pltpu.VMEM((1, particles), F32),
            pltpu.VMEM((ROWS, particles), F32),
            pltpu.VMEM(particle_cell.shape, jnp.int32),
            pltpu.VMEM(les_mean.shape, F32),
            pltpu.VMEM(mix_rate.shape, F32),
            pltpu.VMEM((2 * block_y, particles), BF),
            pltpu.VMEM((2 * ROWS, particles), BF),
            pltpu.VMEM((1, particles), F32),
            pltpu.VMEM((2, (span_x // 2 + 1) * 2 * ROWS, 2 * block_y), F32),
            pltpu.VMEM(tiles, F32),
            pltpu.VMEM((span_x, ROWS, block_y), F32),
            pltpu.VMEM((block_x, ROWS, block_y), F32),
            pltpu.VMEM((2, W + 1, ROWS, LANES), F32),
            pltpu.VMEM((2, ROWS, LANES), F32),
            pltpu.VMEM((2, 2, ROWS, LANES), F32),
            dma((particles // chunk,)), dma((4,)), dma((2,)), dma((2,)), dma((8,)), dma((8,)),
        ],
        compiler_params=pltpu.CompilerParams(
            collective_id=0, has_side_effects=True, vmem_limit_bytes=40 << 20
        ),
    )(*stay)
    piece = 512
    group = 2048
    return pl.pallas_call(
        functools.partial(react_kernel, block_x, block_y, piece, group),
        out_shape=(
            jax.ShapeDtypeStruct(composition.shape, F32),
            jax.ShapeDtypeStruct(les_mean.shape, F32),
        ),
        in_specs=[whole] * 6,
        out_specs=[pl.BlockSpec(memory_space=pl.ANY)] * 2,
        scratch_shapes=[
            pltpu.VMEM((span_x // 2 * ROWS, 4 * block_y), BF),
            pltpu.VMEM((ROWS, LANES), BF),
            pltpu.VMEM((ROWS, particles), F32),
            pltpu.VMEM(composition.shape, F32),
            pltpu.VMEM((ROWS + NS_MID, ROWS + NS_MID), F32),
            pltpu.VMEM((ROWS + NS_MID, ROWS + NS_MID), F32),
            dma((particles // group,)),
            dma(()),
            pltpu.VMEM(les_mean.shape, F32),
            pltpu.VMEM((ROWS, particles), F32),
            pltpu.VMEM((ROWS + NS_MID, 3 * (ROWS + NS_MID)), BF),
            pltpu.VMEM((ROWS + NS_MID, 3 * (ROWS + NS_MID)), BF),
        ],
        compiler_params=pltpu.CompilerParams(vmem_limit_bytes=40 << 20),
    )(composition, particle_cell, particle_level[None], table, rate_matrix, implicit_map)


def solution(mesh):
    placed = (
        P(None, ("gx", "gy")),
        P(("gx", "gy")),
        P(None, ("gx", "gy")),
        P(("gx", "gy")),
        P(None, "gx", "gy"),
        P("gx", "gy"),
        P(),
        P(),
    )
    return jax.shard_map(
        functools.partial(per_device, (mesh.shape["gx"], mesh.shape["gy"])),
        mesh=mesh,
        in_specs=placed,
        out_specs=(P(None, ("gx", "gy")), P(None, "gx", "gy")),
        check_vma=False,
    )
```

time: 17.9 us -> 17.8 us (level)
  the two profiles are of different devices: /device:TPU:19 before, /device:TPU:1 now
where the time goes in v3:
time: 17.8 us; the launch traced here: 17.6 us
  Pallas kernels  16.9 us (95%)
  between operations  0.72 us (4%)
    pallas_call x1, Pallas kernels, per_device(): pl.pallas_call(functools.partial(sums_kernel, counts, chunk, block_x, blo...  11.3 us
    pallas_call x1, Pallas kernels, per_device(): pl.pallas_call(functools.partial(react_kernel, block_x, block_y, piece, g...  5.6 us

profile of v3, /device:TPU:1, one launch (start us, length us, event | category | flops | bytes accessed | tf_op | source)
XLA Modules:
  0.0 17.6 jit_solution(11218258455934363511)
XLA Ops:
  0.6 0.0 copy-start.1
  0.6 0.0 copy-start
  0.7 0.0 copy-start.3
  0.7 0.0 copy-start.2
  0.7 0.0 copy-start.4
  0.7 11.3 %shard_map.95.table = f32[9,56,128]{2,1,0:T(8,128)S(1)} custom-call(f32[53,8192]{1,0:T(8,128)} %comp.3, f32[1,8192]{1,0:T(1,128)} %bitcast.3, s32[2,8192]{1,0:T(2,128)} %cell.1, f32[53,4,128]{2,1,0:T(4,128)} %les_in.1, f32[4,128]{1,0:T(4,128)} %rate_in.1), custom_call_target="tpu_custom_call" | custom-call | tf_op jit(solution)/shard_map/pallas_call | solution.py:470
  12.0 0.0 copy-done.1
  12.0 0.0 copy-done
  12.0 0.0 copy-done.3
  12.0 0.0 copy-done.2
  12.0 0.0 copy-done.4
  12.0 5.6 %shard_map.96 = (f32[53,8192]{1,0:T(8,128)}, f32[53,4,128]{2,1,0:T(4,128)}) custom-call(f32[53,8192]{1,0:T(8,128)S(1)} %copy-done, s32[2,8192]{1,0:T(2,128)S(1)} %copy-done.1, s32[1,8192]{1,0:T(1,128)S(1)} %bitcast.2, f32[9,56,128]{2,1,0:T(8,128)S(1)} %shard_map.95.table, f32[3,53,53]{2,1,0:T(8,128)S(1)} %copy-done.2, f32[3,53,53]{2,1,0:T(8,128)S(1)} %copy-done.3), custom_call_target="tpu_custom_call" | custom-call | tf_op jit(solution)/shard_map/pallas_call | solution.py:500
Async XLA Ops:
  0.6 11.3 %copy-start.1 = (s32[2,8192]{1,0:T(2,128)S(1)}, s32[2,8192]{1,0:T(2,128)}, u32[]{:S(2)}) copy-start(s32[2,8192]{1,0:T(2,128)} %cell.1) | copy-start | bytes 196612
  0.6 11.3 %copy-start = (f32[53,8192]{1,0:T(8,128)S(1)}, f32[53,8192]{1,0:T(8,128)}, u32[]{:S(2)}) copy-start(f32[53,8192]{1,0:T(8,128)} %comp.3) | copy-start | bytes 5210116
  0.7 11.3 %copy-start.3 = (f32[3,53,53]{2,1,0:T(8,128)S(1)}, f32[3,53,53]{2,1,0:T(8,128)}, u32[]{:S(2)}) copy-start(f32[3,53,53]{2,1,0:T(8,128)} %implicit.1) | copy-start | bytes 101128
  0.7 11.3 %copy-start.2 = (f32[3,53,53]{2,1,0:T(8,128)S(1)}, f32[3,53,53]{2,1,0:T(8,128)}, u32[]{:S(2)}) copy-start(f32[3,53,53]{2,1,0:T(8,128)} %rate.1) | copy-start | bytes 101128
  0.7 11.3 %copy-start.4 = (s32[8192]{0:T(1024)S(1)}, s32[8192]{0:T(1024)}, u32[]{:S(2)}) copy-start(s32[8192]{0:T(1024)} %param.11) | copy-start | bytes 98308

commit v4 on v3

--- a/solution.py
+++ b/solution.py
@@ -56,8 +56,8 @@
 
 
 def sums_kernel(
-    counts, chunk, block_x, block_y, comp, mass, cell_in, les_in, rate_in, table,
-    data, weight, weighted, cell, les, rate, hot, both, codes, acc, send, prior, plain, from_x, from_y, from_xy,
+    counts, chunk, piece, block_x, block_y, comp, mass, cell_in, les_in, rate_in, table,
+    data, weight, ending, cell, les, rate, hot, codes, masked, acc, send, prior, plain, from_x, from_y, from_xy,
     comp_sem, small_sem, send_main, recv_main, send_rim, recv_rim,
 ):
     species, particles = comp.shape
@@ -66,6 +66,7 @@
     side_size = span_x * W
     tall = 2 * ROWS
     chunks = particles // chunk
+    base8 = species // 8 * 8
     gx, gy = lax.axis_index("gx"), lax.axis_index("gy")
     upper_first = gx % 2
     has = {
@@ -155,7 +156,7 @@
             pl.semaphore_signal(
                 barrier, inc=1, device_id=(gx + dx, gy + dy), device_id_type=MESH
             )
-    weighted[species:, :] = jnp.zeros((ROWS - species, particles), F32)
+    ending[species - base8 :, :] = jnp.zeros((ROWS - species, particles), F32)
     prior[...] = jnp.zeros_like(prior)
     for dx in (-1, 1):
         @pl.when(jnp.logical_not(has[dx][0]))
@@ -167,48 +168,38 @@
             def _():
                 landing(dx, dy)[...] = jnp.zeros((ROWS, LANES), F32)
 
-    def add_up(start, size, groups, first, fresh):
-        for part in range(2):
-            span = slice(start + part * (size // 2), start + (part + 1) * (size // 2))
-            code = jnp.broadcast_to(codes[:, span], (16, size // 2)).astype(BF)
-            value = both[:, span]
-            rows = []
-            for group in groups:
-                keep = jnp.where(code == group, jnp.ones((), BF), jnp.zeros((), BF))
-                rows.append(value * jnp.concatenate([keep] * (tall // 16), 0))
-            got = lax.dot_general(
-                jnp.concatenate(rows, 0), hot[:, span], (((1,), (1,)), ((), ())),
-                preferred_element_type=F32,
-            )
-            if fresh:
-                acc[part, first : first + len(groups) * tall] = got
-            else:
-                acc[part, first : first + len(groups) * tall] += got
-
     def total_of(at, cols):
         low, high = slice(at, at + ROWS), slice(at + ROWS, at + tall)
-        return (acc[0, low, cols] + acc[1, low, cols]) + (acc[0, high, cols] + acc[1, high, cols])
-
-    def half_tiles(base, first):
-        for u in range(W):
-            cols = slice((u % 2) * block_y, (u % 2 + 1) * block_y)
-            t = first + u
-            send[t] = total_of(base + (u // 2) * tall, cols) + prior[t]
-
-    def prepare(k):
-        for at in range(k * chunk, (k + 1) * chunk, 4 * LANES):
-            span = slice(at, at + 4 * LANES)
-            local_x, on_rim, rim, inner = positions(cell[:, span], block_x, block_y)
-            hot[:, span] = one_hot(
-                jnp.where(on_rim, rim, inner + (local_x % 2) * block_y), 2 * block_y
+        return acc[low, cols] + acc[high, cols]
+
+    def half_tiles(first):
+        for t in range(first, first + W):
+            cols = slice((t % 2) * block_y, (t % 2 + 1) * block_y)
+            send[t] = total_of(t // 2 * tall, cols) + prior[t]
+
+    def place(at):
+        span = slice(at, at + piece)
+        local_x, on_rim, rim, inner = positions(cell[:, span], block_x, block_y)
+        hot[:, span] = one_hot(
+            jnp.where(on_rim, rim, inner + (local_x % 2) * block_y), 2 * block_y
+        )
+        code = jnp.where(on_rim, pairs, local_x // 2)
+        codes[:, span] = code.astype(F32)
+
+    def prepare(at):
+        span = slice(at, at + piece)
+        mass_here = weight[:, span]
+        ending[0 : species - base8, span] = data[base8:, span] * mass_here
+        ending[species - base8 : species - base8 + 1, span] = mass_here
+        value = jnp.concatenate([data[0:base8, span] * mass_here, ending[:, span]], 0)
+        high = value.astype(BF).astype(F32)
+        value = jnp.concatenate([high, value - high], 0).astype(BF)
+        code = jnp.broadcast_to(codes[:, span], (16, piece)).astype(BF)
+        for group in range(pairs + 1):
+            keep = jnp.where(code == group, jnp.ones((), BF), jnp.zeros((), BF))
+            masked[group * tall : (group + 1) * tall, span] = value * jnp.concatenate(
+                [keep] * (tall // 16), 0
             )
-            code = jnp.where(on_rim, pairs, (local_x // 2 + upper_first * (pairs // 2)) % pairs)
-            codes[:, span] = code.astype(F32)
-            weighted[0:species, span] = data[:, span] * weight[:, span]
-            weighted[species : species + 1, span] = weight[:, span]
-            value = weighted[:, span]
-            high = value.astype(BF).astype(F32)
-            both[:, span] = jnp.concatenate([high, value - high], 0).astype(BF)
 
     def set_prior():
         small[2].wait()
@@ -218,26 +209,40 @@
             plain[x] = own
             prior[x + R] = jnp.where(inside, own, 0.0)
 
-    early = list(range(pairs // 2)) + [pairs]
-    late = list(range(pairs // 2, pairs))
     small[0].wait()
+    for at in range(0, particles, piece):
+        place(at)
     small[1].wait()
-    late_at = len(early) * tall
-    chunk_copy(0).wait()
-    prepare(0)
     for k in range(chunks):
-        @pl.when(gx >= 0)
-        def _():
-            if k + 1 < chunks:
-                chunk_copy(k + 1).wait()
-            add_up(k * chunk, chunk, early, 0, k == 0)
-            if k + 1 < chunks:
-                prepare(k + 1)
-            else:
-                set_prior()
-
-    half_tiles(0, upper_first * block_x)
-    rim_sum = total_of((pairs // 2) * tall, slice(0, LANES))
+        chunk_copy(k).wait()
+        for at in range(k * chunk, (k + 1) * chunk, piece):
+            prepare(at)
+
+    set_prior()
+    acc[...] = lax.dot_general(
+        masked[...], hot[...], (((1,), (1,)), ((), ())), preferred_element_type=F32
+    )
+    number = (1 + (gx > 0).astype(jnp.int32) + (gx < counts[0] - 1).astype(jnp.int32)) * (
+        1 + (gy > 0).astype(jnp.int32) + (gy < counts[1] - 1).astype(jnp.int32)
+    ) - 1
+    pl.semaphore_wait(barrier, number)
+
+    def send_half(dx):
+        half_tiles(0 if dx < 0 else block_x)
+
+        @pl.when(has[dx][0])
+        def _():
+            main_copy(dx).start()
+
+    @pl.when(upper_first == 0)
+    def _():
+        send_half(-1)
+
+    @pl.when(upper_first == 1)
+    def _():
+        send_half(1)
+
+    rim_sum = total_of(pairs * tall, slice(0, LANES))
     for x in range(block_x):
         t = x + R
         low_at, high_at = t * W + R, side_size + t * W
@@ -245,37 +250,18 @@
         rim_sum += jnp.where((lane >= low_at) & (lane < low_at + R), low, 0.0)
         rim_sum += jnp.where((lane >= high_at) & (lane < high_at + R), high, 0.0)
     send[span_x] = rim_sum
-    number = (1 + (gx > 0).astype(jnp.int32) + (gx < counts[0] - 1).astype(jnp.int32)) * (
-        1 + (gy > 0).astype(jnp.int32) + (gy < counts[1] - 1).astype(jnp.int32)
-    ) - 1
-    pl.semaphore_wait(barrier, number)
-
-    @pl.when(jnp.logical_and(upper_first == 0, has[-1][0]))
-    def _():
-        main_copy(-1).start()
-
-    @pl.when(jnp.logical_and(upper_first == 1, has[1][0]))
-    def _():
-        main_copy(1).start()
-
     for k, (dx, dy) in enumerate(others):
         @pl.when(present(dx, dy))
         def _():
             rim_copy(k, dx, dy).start()
 
-    @pl.when(gx >= 0)
+    @pl.when(upper_first == 1)
     def _():
-        add_up(0, particles, late, late_at, True)
-
-    half_tiles(late_at, (1 - upper_first) * block_x)
-
-    @pl.when(jnp.logical_and(upper_first == 1, has[-1][0]))
+        send_half(-1)
+
+    @pl.when(upper_first == 0)
     def _():
-        main_copy(-1).start()
-
-    @pl.when(jnp.logical_and(upper_first == 0, has[1][0]))
-    def _():
-        main_copy(1).start()
+        send_half(1)
 
     for k, (dx, dy) in enumerate(others):
         @pl.when(present(dx, dy))
@@ -323,12 +309,12 @@
         for t in range(first, first + W):
             close(t)
 
-    @pl.when(upper_first == 0)
+    @pl.when(upper_first == 1)
     def _():
         close_half(-1)
         close_half(1)
 
-    @pl.when(upper_first == 1)
+    @pl.when(upper_first == 0)
     def _():
         close_half(1)
         close_half(-1)
@@ -468,21 +454,21 @@
     dma = pltpu.SemaphoreType.DMA
     tiles = (span_x + 1, ROWS, LANES)
     table = pl.pallas_call(
-        functools.partial(sums_kernel, counts, chunk, block_x, block_y),
+        functools.partial(sums_kernel, counts, chunk, 512, block_x, block_y),
         out_shape=pltpu.VMEM(tiles, F32),
         in_specs=[hbm] * 5,
         out_specs=whole,
         scratch_shapes=[
             pltpu.VMEM(composition.shape, F32),
             pltpu.VMEM((1, particles), F32),
-            pltpu.VMEM((ROWS, particles), F32),
+            pltpu.VMEM((8, particles), F32),
             pltpu.VMEM(particle_cell.shape, jnp.int32),
             pltpu.VMEM(les_mean.shape, F32),
             pltpu.VMEM(mix_rate.shape, F32),
             pltpu.VMEM((2 * block_y, particles), BF),
-            pltpu.VMEM((2 * ROWS, particles), BF),
             pltpu.VMEM((1, particles), F32),
-            pltpu.VMEM((2, (span_x // 2 + 1) * 2 * ROWS, 2 * block_y), F32),
+            pltpu.VMEM(((span_x // 2 + 1) * 2 * ROWS, particles), BF),
+            pltpu.VMEM(((span_x // 2 + 1) * 2 * ROWS, 2 * block_y), F32),
             pltpu.VMEM(tiles, F32),
             pltpu.VMEM((span_x, ROWS, block_y), F32),
             pltpu.VMEM((block_x, ROWS, block_y), F32),

time: 17.8 us -> 18.3 us (1.028)
  Pallas kernels: 16.9 us -> 17.4 us
    pallas_call x1, Pallas kernels: 11.3 us -> 11.8 us  [per_device(): pl.pallas_call(functools.partial(sums_kernel, counts, chunk, 512, block_x...]
where the time goes in v4:
time: 18.3 us; the launch traced here: 18.1 us
  Pallas kernels  17.4 us (95%)
  between operations  0.72 us (4%)
    pallas_call x1, Pallas kernels, per_device(): pl.pallas_call(functools.partial(sums_kernel, counts, chunk, 512, block_x...  11.8 us
    pallas_call x1, Pallas kernels, per_device(): pl.pallas_call(functools.partial(react_kernel, block_x, block_y, piece, g...  5.59 us

profile of v4, /device:TPU:1, one launch (start us, length us, event | category | flops | bytes accessed | tf_op | source)
XLA Modules:
  0.0 18.1 jit_solution(6736490323175101389)
XLA Ops:
  0.6 0.0 copy-start.1
  0.6 0.0 copy-start
  0.7 0.0 copy-start.3
  0.7 0.0 copy-start.2
  0.7 0.0 copy-start.4
  0.7 11.8 %shard_map.95.table = f32[9,56,128]{2,1,0:T(8,128)S(1)} custom-call(f32[53,8192]{1,0:T(8,128)} %comp.3, f32[1,8192]{1,0:T(1,128)} %bitcast.3, s32[2,8192]{1,0:T(2,128)} %cell.1, f32[53,4,128]{2,1,0:T(4,128)} %les_in.1, f32[4,128]{1,0:T(4,128)} %rate_in.1), custom_call_target="tpu_custom_call" | custom-call | tf_op jit(solution)/shard_map/pallas_call | solution.py:456
  12.5 0.0 copy-done.1
  12.5 0.0 copy-done
  12.5 0.0 copy-done.3
  12.5 0.0 copy-done.2
  12.5 0.0 copy-done.4
  12.6 5.6 %shard_map.96 = (f32[53,8192]{1,0:T(8,128)}, f32[53,4,128]{2,1,0:T(4,128)}) custom-call(f32[53,8192]{1,0:T(8,128)S(1)} %copy-done, s32[2,8192]{1,0:T(2,128)S(1)} %copy-done.1, s32[1,8192]{1,0:T(1,128)S(1)} %bitcast.2, f32[9,56,128]{2,1,0:T(8,128)S(1)} %shard_map.95.table, f32[3,53,53]{2,1,0:T(8,128)S(1)} %copy-done.2, f32[3,53,53]{2,1,0:T(8,128)S(1)} %copy-done.3), custom_call_target="tpu_custom_call" | custom-call | tf_op jit(solution)/shard_map/pallas_call | solution.py:486
Async XLA Ops:
  0.6 11.9 %copy-start.1 = (s32[2,8192]{1,0:T(2,128)S(1)}, s32[2,8192]{1,0:T(2,128)}, u32[]{:S(2)}) copy-start(s32[2,8192]{1,0:T(2,128)} %cell.1) | copy-start | bytes 196612
  0.6 11.9 %copy-start = (f32[53,8192]{1,0:T(8,128)S(1)}, f32[53,8192]{1,0:T(8,128)}, u32[]{:S(2)}) copy-start(f32[53,8192]{1,0:T(8,128)} %comp.3) | copy-start | bytes 5210116
  0.7 11.9 %copy-start.3 = (f32[3,53,53]{2,1,0:T(8,128)S(1)}, f32[3,53,53]{2,1,0:T(8,128)}, u32[]{:S(2)}) copy-start(f32[3,53,53]{2,1,0:T(8,128)} %implicit.1) | copy-start | bytes 101128
  0.7 11.9 %copy-start.2 = (f32[3,53,53]{2,1,0:T(8,128)S(1)}, f32[3,53,53]{2,1,0:T(8,128)}, u32[]{:S(2)}) copy-start(f32[3,53,53]{2,1,0:T(8,128)} %rate.1) | copy-start | bytes 101128
  0.7 11.9 %copy-start.4 = (s32[8192]{0:T(1024)S(1)}, s32[8192]{0:T(1024)}, u32[]{:S(2)}) copy-start(s32[8192]{0:T(1024)} %param.11) | copy-start | bytes 98308

commit v5 on v4

--- a/solution.py
+++ b/solution.py
@@ -14,6 +14,7 @@
 HALF = 64
 ROWS = 56
 LANES = 128
+FOLD = 16
 
 prior_weight = 16.0
 chem_step = 0.5
@@ -56,14 +57,15 @@
 
 
 def sums_kernel(
-    counts, chunk, piece, block_x, block_y, comp, mass, cell_in, les_in, rate_in, table,
-    data, weight, ending, cell, les, rate, hot, codes, masked, acc, send, prior, plain, from_x, from_y, from_xy,
+    counts, chunk, piece, block_x, block_y, comp, mass, cell_in, les_in, rate_in, table, data, cell,
+    weight, ending, les, rate, hot, codes, masked, acc, send, edge, prior, plain, from_x, rim_x, from_y, from_xy,
     comp_sem, small_sem, send_main, recv_main, send_rim, recv_rim,
 ):
     species, particles = comp.shape
     span_x = block_x + 2 * R
     pairs = span_x // 2
     side_size = span_x * W
+    folds = LANES // side_size
     tall = 2 * ROWS
     chunks = particles // chunk
     base8 = species // 8 * 8
@@ -103,7 +105,7 @@
 
     def landing(dx, dy):
         if dy == 0:
-            return from_x.at[(dx + 1) // 2, W]
+            return rim_x.at[(dx + 1) // 2]
         if dx == 0:
             return from_y.at[(dy + 1) // 2]
         return from_xy.at[(dx + 1) // 2, (dy + 1) // 2]
@@ -121,7 +123,7 @@
 
     def rim_copy(k, dx, dy):
         return pltpu.make_async_remote_copy(
-            src_ref=send.at[span_x],
+            src_ref=edge if dy == 0 else edge.at[(dy + 1) // 2],
             dst_ref=landing(-dx, -dy),
             send_sem=send_rim.at[k],
             recv_sem=recv_rim.at[len(others) - 1 - k],
@@ -141,7 +143,7 @@
 
     def rim_arrival(k, dx, dy):
         return pltpu.make_async_remote_copy(
-            src_ref=send.at[span_x],
+            src_ref=edge if dy == 0 else edge.at[(dy + 1) // 2],
             dst_ref=landing(dx, dy),
             send_sem=send_rim.at[k],
             recv_sem=recv_rim.at[k],
@@ -161,12 +163,11 @@
     for dx in (-1, 1):
         @pl.when(jnp.logical_not(has[dx][0]))
         def _():
-            from_x[(dx + 1) // 2] = jnp.zeros((W + 1, ROWS, LANES), F32)
+            from_x[(dx + 1) // 2] = jnp.zeros((W, ROWS, LANES), F32)
     for dx, dy in others:
-        if dy != 0:
-            @pl.when(jnp.logical_not(present(dx, dy)))
-            def _():
-                landing(dx, dy)[...] = jnp.zeros((ROWS, LANES), F32)
+        @pl.when(jnp.logical_not(present(dx, dy)))
+        def _():
+            landing(dx, dy)[...] = jnp.zeros(landing(dx, dy).shape, F32)
 
     def total_of(at, cols):
         low, high = slice(at, at + ROWS), slice(at + ROWS, at + tall)
@@ -249,7 +250,14 @@
         low, high = roll(plain[x], low_at), roll(plain[x], high_at + R)
         rim_sum += jnp.where((lane >= low_at) & (lane < low_at + R), low, 0.0)
         rim_sum += jnp.where((lane >= high_at) & (lane < high_at + R), high, 0.0)
-    send[span_x] = rim_sum
+    rim_sum = jnp.concatenate([rim_sum, jnp.zeros((folds * FOLD - ROWS, LANES), F32)], 0)
+    fold_lane = lax.broadcasted_iota(jnp.int32, (FOLD, LANES), 1)
+    for side in range(2):
+        packed = jnp.zeros((FOLD, LANES), F32)
+        for q in range(folds):
+            moved = roll(rim_sum[q * FOLD : (q + 1) * FOLD], (q - side) * side_size)
+            packed = jnp.where(fold_lane // side_size == q, moved, packed)
+        edge[side] = packed
     for k, (dx, dy) in enumerate(others):
         @pl.when(present(dx, dy))
         def _():
@@ -274,18 +282,28 @@
         weight = jnp.broadcast_to(weight, total.shape)
         return total / jnp.where(row < species, weight, 1.0)
 
-    low_side = lane < side_size
-    place_x = jnp.where(low_side, lane, lane - side_size)
-    used = lane < 2 * side_size
-    behind = used & (place_x < 2 * R * W)
-    ahead = used & (place_x >= block_x * W)
-    total = send[span_x]
-    for dx, dy in others:
-        mask = used if dx == 0 else behind if dx < 0 else ahead
-        if dy != 0:
-            mask = mask & (low_side if dy < 0 else jnp.logical_not(low_side))
-        shift = dx * block_x * W + dy * side_size
-        total = total + jnp.where(mask, roll(landing(dx, dy)[...], shift), 0.0)
+    place_x = fold_lane % side_size
+    sides = []
+    for side in range(2):
+        total = edge[side]
+        for dx, dy in others:
+            if dy == 0:
+                other = rim_x[(dx + 1) // 2, side]
+            elif (dy + 1) // 2 == side:
+                other = landing(dx, dy)[...]
+            else:
+                continue
+            if dx < 0:
+                other = jnp.where(place_x < 2 * R * W, roll(other, dx * block_x * W), 0.0)
+            if dx > 0:
+                other = jnp.where(place_x >= block_x * W, roll(other, dx * block_x * W), 0.0)
+            total = total + other
+        sides.append(total)
+    parts = []
+    for q in range(folds):
+        low, high = roll(sides[0], -q * side_size), roll(sides[1], (1 - q) * side_size)
+        parts.append(jnp.where(fold_lane < side_size, low, high))
+    total = jnp.where(lane < 2 * side_size, jnp.concatenate(parts, 0)[0:ROWS], 0.0)
     rim_value = finish(total)
     table[span_x] = rim_value
 
@@ -453,28 +471,32 @@
     stay = [pltpu.with_memory_space_constraint(x, pltpu.HBM) for x in inputs]
     dma = pltpu.SemaphoreType.DMA
     tiles = (span_x + 1, ROWS, LANES)
-    table = pl.pallas_call(
+    table, composition, particle_cell = pl.pallas_call(
         functools.partial(sums_kernel, counts, chunk, 512, block_x, block_y),
-        out_shape=pltpu.VMEM(tiles, F32),
+        out_shape=(
+            pltpu.VMEM(tiles, F32),
+            pltpu.VMEM(composition.shape, F32),
+            pltpu.VMEM(particle_cell.shape, jnp.int32),
+        ),
         in_specs=[hbm] * 5,
-        out_specs=whole,
+        out_specs=[whole] * 3,
         scratch_shapes=[
-            pltpu.VMEM(composition.shape, F32),
             pltpu.VMEM((1, particles), F32),
             pltpu.VMEM((8, particles), F32),
-            pltpu.VMEM(particle_cell.shape, jnp.int32),
             pltpu.VMEM(les_mean.shape, F32),
             pltpu.VMEM(mix_rate.shape, F32),
             pltpu.VMEM((2 * block_y, particles), BF),
             pltpu.VMEM((1, particles), F32),
             pltpu.VMEM(((span_x // 2 + 1) * 2 * ROWS, particles), BF),
             pltpu.VMEM(((span_x // 2 + 1) * 2 * ROWS, 2 * block_y), F32),
-            pltpu.VMEM(tiles, F32),
+            pltpu.VMEM((span_x, ROWS, LANES), F32),
+            pltpu.VMEM((2, FOLD, LANES), F32),
             pltpu.VMEM((span_x, ROWS, block_y), F32),
             pltpu.VMEM((block_x, ROWS, block_y), F32),
-            pltpu.VMEM((2, W + 1, ROWS, LANES), F32),
-            pltpu.VMEM((2, ROWS, LANES), F32),
-            pltpu.VMEM((2, 2, ROWS, LANES), F32),
+            pltpu.VMEM((2, W, ROWS, LANES), F32),
+            pltpu.VMEM((2, 2, FOLD, LANES), F32),
+            pltpu.VMEM((2, FOLD, LANES), F32),
+            pltpu.VMEM((2, 2, FOLD, LANES), F32),
             dma((particles // chunk,)), dma((4,)), dma((2,)), dma((2,)), dma((8,)), dma((8,)),
         ],
         compiler_params=pltpu.CompilerParams(

time: 18.3 us -> 17.5 us (0.956)
  Pallas kernels: 17.4 us -> 16.7 us
    pallas_call x1, Pallas kernels: 11.8 us -> 11.1 us  [per_device(): pl.pallas_call(functools.partial(sums_kernel, counts, chunk, 512, block_x...]
where the time goes in v5:
time: 17.5 us; the launch traced here: 17.4 us
  Pallas kernels  16.7 us (95%)
  between operations  0.69 us (4%)
    pallas_call x1, Pallas kernels, per_device(): pl.pallas_call(functools.partial(sums_kernel, counts, chunk, 512, block_x...  11.1 us
    pallas_call x1, Pallas kernels, per_device(): pl.pallas_call(functools.partial(react_kernel, block_x, block_y, piece, g...  5.63 us

profile of v5, /device:TPU:1, one launch (start us, length us, event | category | flops | bytes accessed | tf_op | source)
XLA Modules:
  0.0 17.4 jit_solution(8020106617708232908)
XLA Ops:
  0.6 0.0 copy-start.1
  0.6 0.0 copy-start
  0.7 0.0 copy-start.2
  0.7 11.1 %shard_map.95 = (f32[9,56,128]{2,1,0:T(8,128)S(1)}, f32[53,8192]{1,0:T(8,128)S(1)}, s32[2,8192]{1,0:T(2,128)S(1)}) custom-call(f32[53,8192]{1,0:T(8,128)} %comp.1, f32[1,8192]{1,0:T(1,128)} %bitcast.3, s32[2,8192]{1,0:T(2,128)} %cell_in.1, f32[53,4,128]{2,1,0:T(4,128)} %les_in.1, f32[4,128]{1,0:T(4,128)} %rate_in.1), custom_call_target="tpu_custom_call" | custom-call | tf_op jit(solution)/shard_map/pallas_call | solution.py:474
  11.7 0.0 copy-done.1
  11.7 0.0 copy-done
  11.7 0.0 copy-done.2
  11.8 5.6 %shard_map.96 = (f32[53,8192]{1,0:T(8,128)}, f32[53,4,128]{2,1,0:T(4,128)}) custom-call(f32[53,8192]{1,0:T(8,128)S(1)} %get-tuple-element.5.comp, s32[2,8192]{1,0:T(2,128)S(1)} %get-tuple-element.6.cell, s32[1,8192]{1,0:T(1,128)S(1)} %bitcast.2, f32[9,56,128]{2,1,0:T(8,128)S(1)} %get-tuple-element.7.table, f32[3,53,53]{2,1,0:T(8,128)S(1)} %copy-done, ...), custom_call_target="tpu_custom_call" | custom-call | tf_op jit(solution)/shard_map/pallas_call | solution.py:508
Async XLA Ops:
  0.6 11.1 %copy-start.1 = (f32[3,53,53]{2,1,0:T(8,128)S(1)}, f32[3,53,53]{2,1,0:T(8,128)}, u32[]{:S(2)}) copy-start(f32[3,53,53]{2,1,0:T(8,128)} %implicit.1) | copy-start | bytes 101128
  0.6 11.1 %copy-start = (f32[3,53,53]{2,1,0:T(8,128)S(1)}, f32[3,53,53]{2,1,0:T(8,128)}, u32[]{:S(2)}) copy-start(f32[3,53,53]{2,1,0:T(8,128)} %rate.1) | copy-start | bytes 101128
  0.7 11.1 %copy-start.2 = (s32[8192]{0:T(1024)S(1)}, s32[8192]{0:T(1024)}, u32[]{:S(2)}) copy-start(s32[8192]{0:T(1024)} %param.11) | copy-start | bytes 98308

commit v6 on v5

--- a/solution.py
+++ b/solution.py
@@ -69,6 +69,9 @@
     tall = 2 * ROWS
     chunks = particles // chunk
     base8 = species // 8 * 8
+    early = list(range(pairs // 2)) + [pairs]
+    late = list(range(pairs // 2, pairs))
+    rows = len(early) * tall
     gx, gy = lax.axis_index("gx"), lax.axis_index("gy")
     upper_first = gx % 2
     has = {
@@ -160,6 +163,7 @@
             )
     ending[species - base8 :, :] = jnp.zeros((ROWS - species, particles), F32)
     prior[...] = jnp.zeros_like(prior)
+    masked[2 * rows - tall :, :] = jnp.zeros((tall, particles), BF)
     for dx in (-1, 1):
         @pl.when(jnp.logical_not(has[dx][0]))
         def _():
@@ -174,9 +178,9 @@
         return acc[low, cols] + acc[high, cols]
 
     def half_tiles(first):
-        for t in range(first, first + W):
-            cols = slice((t % 2) * block_y, (t % 2 + 1) * block_y)
-            send[t] = total_of(t // 2 * tall, cols) + prior[t]
+        for u in range(W):
+            cols = slice((u % 2) * block_y, (u % 2 + 1) * block_y)
+            send[first + u] = total_of(u // 2 * tall, cols) + prior[first + u]
 
     def place(at):
         span = slice(at, at + piece)
@@ -184,7 +188,7 @@
         hot[:, span] = one_hot(
             jnp.where(on_rim, rim, inner + (local_x % 2) * block_y), 2 * block_y
         )
-        code = jnp.where(on_rim, pairs, local_x // 2)
+        code = jnp.where(on_rim, pairs, (local_x // 2 + upper_first * (pairs // 2)) % pairs)
         codes[:, span] = code.astype(F32)
 
     def prepare(at):
@@ -196,9 +200,9 @@
         high = value.astype(BF).astype(F32)
         value = jnp.concatenate([high, value - high], 0).astype(BF)
         code = jnp.broadcast_to(codes[:, span], (16, piece)).astype(BF)
-        for group in range(pairs + 1):
+        for i, group in enumerate(early + late):
             keep = jnp.where(code == group, jnp.ones((), BF), jnp.zeros((), BF))
-            masked[group * tall : (group + 1) * tall, span] = value * jnp.concatenate(
+            masked[i * tall : (i + 1) * tall, span] = value * jnp.concatenate(
                 [keep] * (tall // 16), 0
             )
 
@@ -220,56 +224,49 @@
             prepare(at)
 
     set_prior()
-    acc[...] = lax.dot_general(
-        masked[...], hot[...], (((1,), (1,)), ((), ())), preferred_element_type=F32
-    )
     number = (1 + (gx > 0).astype(jnp.int32) + (gx < counts[0] - 1).astype(jnp.int32)) * (
         1 + (gy > 0).astype(jnp.int32) + (gy < counts[1] - 1).astype(jnp.int32)
     ) - 1
-    pl.semaphore_wait(barrier, number)
-
-    def send_half(dx):
-        half_tiles(0 if dx < 0 else block_x)
-
-        @pl.when(has[dx][0])
-        def _():
-            main_copy(dx).start()
-
-    @pl.when(upper_first == 0)
-    def _():
-        send_half(-1)
-
-    @pl.when(upper_first == 1)
-    def _():
-        send_half(1)
-
-    rim_sum = total_of(pairs * tall, slice(0, LANES))
-    for x in range(block_x):
-        t = x + R
-        low_at, high_at = t * W + R, side_size + t * W
-        low, high = roll(plain[x], low_at), roll(plain[x], high_at + R)
-        rim_sum += jnp.where((lane >= low_at) & (lane < low_at + R), low, 0.0)
-        rim_sum += jnp.where((lane >= high_at) & (lane < high_at + R), high, 0.0)
-    rim_sum = jnp.concatenate([rim_sum, jnp.zeros((folds * FOLD - ROWS, LANES), F32)], 0)
-    fold_lane = lax.broadcasted_iota(jnp.int32, (FOLD, LANES), 1)
-    for side in range(2):
-        packed = jnp.zeros((FOLD, LANES), F32)
-        for q in range(folds):
-            moved = roll(rim_sum[q * FOLD : (q + 1) * FOLD], (q - side) * side_size)
-            packed = jnp.where(fold_lane // side_size == q, moved, packed)
-        edge[side] = packed
-    for k, (dx, dy) in enumerate(others):
-        @pl.when(present(dx, dy))
-        def _():
-            rim_copy(k, dx, dy).start()
-
-    @pl.when(upper_first == 1)
-    def _():
-        send_half(-1)
-
-    @pl.when(upper_first == 0)
-    def _():
-        send_half(1)
+
+    @pl.loop(0, 2)
+    def _(phase):
+        top = pl.ds(pl.multiple_of(phase * rows, 16), rows)
+        acc[...] = lax.dot_general(
+            masked[top, :], hot[...], (((1,), (1,)), ((), ())), preferred_element_type=F32
+        )
+        half = (phase + upper_first) % 2
+        half_tiles(half * block_x)
+
+        @pl.when(phase == 0)
+        def _():
+            pl.semaphore_wait(barrier, number)
+
+        for dx in (-1, 1):
+            @pl.when(jnp.logical_and(half == (dx + 1) // 2, has[dx][0]))
+            def _():
+                main_copy(dx).start()
+
+        @pl.when(phase == 0)
+        def _():
+            rim_sum = total_of(pairs // 2 * tall, slice(0, LANES))
+            for x in range(block_x):
+                t = x + R
+                low_at, high_at = t * W + R, side_size + t * W
+                low, high = roll(plain[x], low_at), roll(plain[x], high_at + R)
+                rim_sum += jnp.where((lane >= low_at) & (lane < low_at + R), low, 0.0)
+                rim_sum += jnp.where((lane >= high_at) & (lane < high_at + R), high, 0.0)
+            rim_sum = jnp.concatenate([rim_sum, jnp.zeros((folds * FOLD - ROWS, LANES), F32)], 0)
+            fold_lane = lax.broadcasted_iota(jnp.int32, (FOLD, LANES), 1)
+            for side in range(2):
+                packed = jnp.zeros((FOLD, LANES), F32)
+                for q in range(folds):
+                    moved = roll(rim_sum[q * FOLD : (q + 1) * FOLD], (q - side) * side_size)
+                    packed = jnp.where(fold_lane // side_size == q, moved, packed)
+                edge[side] = packed
+            for k, (dx, dy) in enumerate(others):
+                @pl.when(present(dx, dy))
+                def _():
+                    rim_copy(k, dx, dy).start()
 
     for k, (dx, dy) in enumerate(others):
         @pl.when(present(dx, dy))
@@ -282,6 +279,7 @@
         weight = jnp.broadcast_to(weight, total.shape)
         return total / jnp.where(row < species, weight, 1.0)
 
+    fold_lane = lax.broadcasted_iota(jnp.int32, (FOLD, LANES), 1)
     place_x = fold_lane % side_size
     sides = []
     for side in range(2):
@@ -487,8 +485,8 @@
             pltpu.VMEM(mix_rate.shape, F32),
             pltpu.VMEM((2 * block_y, particles), BF),
             pltpu.VMEM((1, particles), F32),
-            pltpu.VMEM(((span_x // 2 + 1) * 2 * ROWS, particles), BF),
-            pltpu.VMEM(((span_x // 2 + 1) * 2 * ROWS, 2 * block_y), F32),
+            pltpu.VMEM(((span_x // 2 + 2) * 2 * ROWS, particles), BF),
+            pltpu.VMEM(((span_x // 4 + 1) * 2 * ROWS, 2 * block_y), F32),
             pltpu.VMEM((span_x, ROWS, LANES), F32),
             pltpu.VMEM((2, FOLD, LANES), F32),
             pltpu.VMEM((span_x, ROWS, block_y), F32),

time: 17.5 us -> 17.3 us (0.989)
  Pallas kernels: 16.7 us -> 16.5 us
where the time goes in v6:
time: 17.3 us; the launch traced here: 17.2 us
  Pallas kernels  16.5 us (95%)
  between operations  0.69 us (4%)
    pallas_call x1, Pallas kernels, per_device(): pl.pallas_call(functools.partial(sums_kernel, counts, chunk, 512, block_x...  10.9 us
    pallas_call x1, Pallas kernels, per_device(): pl.pallas_call(functools.partial(react_kernel, block_x, block_y, piece, g...  5.59 us

profile of v6, /device:TPU:1, one launch (start us, length us, event | category | flops | bytes accessed | tf_op | source)
XLA Modules:
  0.0 17.2 jit_solution(13816528963332435320)
XLA Ops:
  0.6 0.0 copy-start.1
  0.6 0.0 copy-start
  0.7 0.0 copy-start.2
  0.7 10.9 %shard_map.95 = (f32[9,56,128]{2,1,0:T(8,128)S(1)}, f32[53,8192]{1,0:T(8,128)S(1)}, s32[2,8192]{1,0:T(2,128)S(1)}) custom-call(f32[53,8192]{1,0:T(8,128)} %comp.1, f32[1,8192]{1,0:T(1,128)} %bitcast.3, s32[2,8192]{1,0:T(2,128)} %cell_in.1, f32[53,4,128]{2,1,0:T(4,128)} %les_in.1, f32[4,128]{1,0:T(4,128)} %rate_in.1), custom_call_target="tpu_custom_call" | custom-call | tf_op jit(solution)/shard_map/pallas_call | solution.py:472
  11.6 0.0 copy-done.1
  11.6 0.0 copy-done
  11.6 0.0 copy-done.2
  11.6 5.6 %shard_map.96 = (f32[53,8192]{1,0:T(8,128)}, f32[53,4,128]{2,1,0:T(4,128)}) custom-call(f32[53,8192]{1,0:T(8,128)S(1)} %get-tuple-element.5.comp, s32[2,8192]{1,0:T(2,128)S(1)} %get-tuple-element.6.cell, s32[1,8192]{1,0:T(1,128)S(1)} %bitcast.2, f32[9,56,128]{2,1,0:T(8,128)S(1)} %get-tuple-element.7.table, f32[3,53,53]{2,1,0:T(8,128)S(1)} %copy-done, ...), custom_call_target="tpu_custom_call" | custom-call | tf_op jit(solution)/shard_map/pallas_call | solution.py:506
Async XLA Ops:
  0.6 10.9 %copy-start.1 = (f32[3,53,53]{2,1,0:T(8,128)S(1)}, f32[3,53,53]{2,1,0:T(8,128)}, u32[]{:S(2)}) copy-start(f32[3,53,53]{2,1,0:T(8,128)} %implicit.1) | copy-start | bytes 101128
  0.6 10.9 %copy-start = (f32[3,53,53]{2,1,0:T(8,128)S(1)}, f32[3,53,53]{2,1,0:T(8,128)}, u32[]{:S(2)}) copy-start(f32[3,53,53]{2,1,0:T(8,128)} %rate.1) | copy-start | bytes 101128
  0.7 10.9 %copy-start.2 = (s32[8192]{0:T(1024)S(1)}, s32[8192]{0:T(1024)}, u32[]{:S(2)}) copy-start(s32[8192]{0:T(1024)} %param.11) | copy-start | bytes 98308

commit v7 on v6

--- a/solution.py
+++ b/solution.py
@@ -14,6 +14,7 @@
 HALF = 64
 ROWS = 56
 LANES = 128
+STACK = 112
 FOLD = 16
 
 prior_weight = 16.0
@@ -325,12 +326,12 @@
         for t in range(first, first + W):
             close(t)
 
-    @pl.when(upper_first == 1)
+    @pl.when(upper_first == 0)
     def _():
         close_half(-1)
         close_half(1)
 
-    @pl.when(upper_first == 0)
+    @pl.when(upper_first == 1)
     def _():
         close_half(1)
         close_half(-1)
@@ -349,10 +350,11 @@
     species = matrices.shape[1]
     plain[...] = jnp.zeros_like(plain)
     plain[0:species, 0:species] = matrices[2]
-    plain[0:NS_MID, ROWS : ROWS + NS_MID] = matrices[1, 0:NS_MID, 0:NS_MID]
-    plain[ROWS : ROWS + NS_LOW, ROWS : ROWS + NS_LOW] = matrices[0, 0:NS_LOW, 0:NS_LOW]
-    high, low = halves(plain[...])
-    return jnp.concatenate([high, high, low], 1)
+    plain[ROWS : ROWS + NS_MID, 0:NS_MID] = matrices[1, 0:NS_MID, 0:NS_MID]
+    base = ROWS + NS_MID
+    plain[base : base + NS_LOW, 0:NS_LOW] = matrices[0, 0:NS_LOW, 0:NS_LOW]
+    high = plain[...].astype(BF).astype(F32)
+    return jnp.concatenate([high, high, plain[...] - high], 1).astype(BF)
 
 
 def react_kernel(
@@ -382,16 +384,13 @@
         shape = (yes.shape[0] // 8, 8, piece)
         return jnp.where(test[None], yes.reshape(shape), no.reshape(shape)).reshape(yes.shape)
 
-    def act(matrix, value, full, middle):
-        zero = jnp.zeros_like(value)
-        slots = jnp.concatenate(
-            [choose(full, value, zero), choose(full, zero[0:NS_MID], value[0:NS_MID])], 0
-        )
-        high, low = halves(slots)
-        right = jnp.concatenate([high, low, high], 0)
+    def act(matrix, value, full, lowest):
+        high = value.astype(BF).astype(F32)
+        right = jnp.concatenate([high, value - high, high], 0).astype(BF)
         got = jnp.dot(matrix, right, preferred_element_type=F32)
-        first = choose(middle, got[ROWS:], got[0:NS_MID])
-        return jnp.concatenate([first, got[NS_MID:ROWS]], 0)
+        base = ROWS + NS_MID
+        first = choose(lowest, got[base : base + NS_MID], got[ROWS:base])
+        return choose(full, got[0:NS_MID], first), got[NS_MID:ROWS]
 
     def copy(k):
         span = pl.ds(k * group, group)
@@ -427,11 +426,14 @@
         return levels == 2, levels == 0
 
     def drive(span):
-        source[:, span] = jnp.tanh(act(left_rate[...], mixed[:, span], *tests(span)))
+        first, rest = act(left_rate[...], mixed[:, span], *tests(span))
+        source[:, span] = jnp.tanh(jnp.concatenate([first, rest], 0))
 
     def finish(span):
-        change = act(left_implicit[...], source[:, span], *tests(span))
-        updated = mixed[:, span] + chem_step * change
+        full, lowest = tests(span)
+        first, rest = act(left_implicit[...], source[:, span], full, lowest)
+        rest = choose(full, rest, jnp.zeros_like(rest))
+        updated = mixed[:, span] + chem_step * jnp.concatenate([first, rest], 0)
         result[:, span] = updated[0:species]
 
     count = particles // piece
@@ -516,14 +518,14 @@
             pltpu.VMEM((ROWS, LANES), BF),
             pltpu.VMEM((ROWS, particles), F32),
             pltpu.VMEM(composition.shape, F32),
-            pltpu.VMEM((ROWS + NS_MID, ROWS + NS_MID), F32),
-            pltpu.VMEM((ROWS + NS_MID, ROWS + NS_MID), F32),
+            pltpu.VMEM((STACK, ROWS), F32),
+            pltpu.VMEM((STACK, ROWS), F32),
             dma((particles // group,)),
             dma(()),
             pltpu.VMEM(les_mean.shape, F32),
             pltpu.VMEM((ROWS, particles), F32),
-            pltpu.VMEM((ROWS + NS_MID, 3 * (ROWS + NS_MID)), BF),
-            pltpu.VMEM((ROWS + NS_MID, 3 * (ROWS + NS_MID)), BF),
+            pltpu.VMEM((STACK, 3 * ROWS), BF),
+            pltpu.VMEM((STACK, 3 * ROWS), BF),
         ],
         compiler_params=pltpu.CompilerParams(vmem_limit_bytes=40 << 20),
     )(composition, particle_cell, particle_level[None], table, rate_matrix, implicit_map)

time: 17.3 us -> 16.5 us (0.954)
  Pallas kernels: 16.5 us -> 15.6 us
    pallas_call x1, Pallas kernels: 5.59 us -> 4.75 us  [per_device(): pl.pallas_call(functools.partial(react_kernel, block_x, block_y, piece, g...]
where the time goes in v7:
time: 16.5 us; the launch traced here: 16.3 us
  Pallas kernels  15.6 us (95%)
  between operations  0.69 us (4%)
    pallas_call x1, Pallas kernels, per_device(): pl.pallas_call(functools.partial(sums_kernel, counts, chunk, 512, block_x...  10.9 us
    pallas_call x1, Pallas kernels, per_device(): pl.pallas_call(functools.partial(react_kernel, block_x, block_y, piece, g...  4.75 us

profile of v7, /device:TPU:1, one launch (start us, length us, event | category | flops | bytes accessed | tf_op | source)
XLA Modules:
  0.0 16.3 jit_solution(8641393501836392952)
XLA Ops:
  0.6 0.0 copy-start.1
  0.6 0.0 copy-start
  0.7 0.0 copy-start.2
  0.7 10.9 %shard_map.95 = (f32[9,56,128]{2,1,0:T(8,128)S(1)}, f32[53,8192]{1,0:T(8,128)S(1)}, s32[2,8192]{1,0:T(2,128)S(1)}) custom-call(f32[53,8192]{1,0:T(8,128)} %comp.1, f32[1,8192]{1,0:T(1,128)} %bitcast.3, s32[2,8192]{1,0:T(2,128)} %cell_in.1, f32[53,4,128]{2,1,0:T(4,128)} %les_in.1, f32[4,128]{1,0:T(4,128)} %rate_in.1), custom_call_target="tpu_custom_call" | custom-call | tf_op jit(solution)/shard_map/pallas_call | solution.py:474
  11.6 0.0 copy-done.1
  11.6 0.0 copy-done
  11.6 0.0 copy-done.2
  11.6 4.7 %shard_map.96 = (f32[53,8192]{1,0:T(8,128)}, f32[53,4,128]{2,1,0:T(4,128)}) custom-call(f32[53,8192]{1,0:T(8,128)S(1)} %get-tuple-element.5.comp, s32[2,8192]{1,0:T(2,128)S(1)} %get-tuple-element.6.cell, s32[1,8192]{1,0:T(1,128)S(1)} %bitcast.2, f32[9,56,128]{2,1,0:T(8,128)S(1)} %get-tuple-element.7.table, f32[3,53,53]{2,1,0:T(8,128)S(1)} %copy-done, ...), custom_call_target="tpu_custom_call" | custom-call | tf_op jit(solution)/shard_map/pallas_call | solution.py:508
Async XLA Ops:
  0.6 10.9 %copy-start.1 = (f32[3,53,53]{2,1,0:T(8,128)S(1)}, f32[3,53,53]{2,1,0:T(8,128)}, u32[]{:S(2)}) copy-start(f32[3,53,53]{2,1,0:T(8,128)} %implicit.1) | copy-start | bytes 101128
  0.6 10.9 %copy-start = (f32[3,53,53]{2,1,0:T(8,128)S(1)}, f32[3,53,53]{2,1,0:T(8,128)}, u32[]{:S(2)}) copy-start(f32[3,53,53]{2,1,0:T(8,128)} %rate.1) | copy-start | bytes 101128
  0.7 10.9 %copy-start.2 = (s32[8192]{0:T(1024)S(1)}, s32[8192]{0:T(1024)}, u32[]{:S(2)}) copy-start(s32[8192]{0:T(1024)} %param.11) | copy-start | bytes 98308

commit v8 on v7

--- a/solution.py
+++ b/solution.py
@@ -70,11 +70,10 @@
     tall = 2 * ROWS
     chunks = particles // chunk
     base8 = species // 8 * 8
-    early = list(range(pairs // 2)) + [pairs]
-    late = list(range(pairs // 2, pairs))
+    early = list(range(0, pairs, 2)) + [pairs]
+    late = list(range(1, pairs, 2))
     rows = len(early) * tall
     gx, gy = lax.axis_index("gx"), lax.axis_index("gy")
-    upper_first = gx % 2
     has = {
         -1: (gx > 0, gy > 0),
         1: (gx < counts[0] - 1, gy < counts[1] - 1),
@@ -114,13 +113,13 @@
             return from_y.at[(dy + 1) // 2]
         return from_xy.at[(dx + 1) // 2, (dy + 1) // 2]
 
-    def main_copy(dx):
+    def main_copy(dx, phase):
         first = 0 if dx < 0 else block_x
         return pltpu.make_async_remote_copy(
-            src_ref=send.at[pl.ds(first, W)],
-            dst_ref=from_x.at[(1 - dx) // 2, pl.ds(0, W)],
-            send_sem=send_main.at[(dx + 1) // 2],
-            recv_sem=recv_main.at[(1 - dx) // 2],
+            src_ref=send.at[pl.ds(first + R * phase, R)],
+            dst_ref=from_x.at[(1 - dx) // 2, pl.ds(R * phase, R)],
+            send_sem=send_main.at[(dx + 1) // 2, phase],
+            recv_sem=recv_main.at[(1 - dx) // 2, phase],
             device_id=(gx + dx, gy),
             device_id_type=MESH,
         )
@@ -135,12 +134,12 @@
             device_id_type=MESH,
         )
 
-    def main_arrival(dx):
+    def main_arrival(dx, phase):
         return pltpu.make_async_remote_copy(
-            src_ref=send.at[pl.ds(0, W)],
-            dst_ref=from_x.at[(dx + 1) // 2, pl.ds(0, W)],
-            send_sem=send_main.at[(dx + 1) // 2],
-            recv_sem=recv_main.at[(dx + 1) // 2],
+            src_ref=send.at[pl.ds(R * phase, R)],
+            dst_ref=from_x.at[(dx + 1) // 2, pl.ds(R * phase, R)],
+            send_sem=send_main.at[(dx + 1) // 2, phase],
+            recv_sem=recv_main.at[(dx + 1) // 2, phase],
             device_id=(gx + dx, gy),
             device_id_type=MESH,
         )
@@ -178,10 +177,11 @@
         low, high = slice(at, at + ROWS), slice(at + ROWS, at + tall)
         return acc[low, cols] + acc[high, cols]
 
-    def half_tiles(first):
+    def phase_tiles(phase):
         for u in range(W):
             cols = slice((u % 2) * block_y, (u % 2 + 1) * block_y)
-            send[first + u] = total_of(u // 2 * tall, cols) + prior[first + u]
+            t = u // 2 * block_x + R * phase + u % 2
+            send[t] = total_of(u // 2 * tall, cols) + prior[t]
 
     def place(at):
         span = slice(at, at + piece)
@@ -189,7 +189,7 @@
         hot[:, span] = one_hot(
             jnp.where(on_rim, rim, inner + (local_x % 2) * block_y), 2 * block_y
         )
-        code = jnp.where(on_rim, pairs, (local_x // 2 + upper_first * (pairs // 2)) % pairs)
+        code = jnp.where(on_rim, pairs, local_x // 2)
         codes[:, span] = code.astype(F32)
 
     def prepare(at):
@@ -235,17 +235,16 @@
         acc[...] = lax.dot_general(
             masked[top, :], hot[...], (((1,), (1,)), ((), ())), preferred_element_type=F32
         )
-        half = (phase + upper_first) % 2
-        half_tiles(half * block_x)
+        phase_tiles(phase)
 
         @pl.when(phase == 0)
         def _():
             pl.semaphore_wait(barrier, number)
 
         for dx in (-1, 1):
-            @pl.when(jnp.logical_and(half == (dx + 1) // 2, has[dx][0]))
+            @pl.when(has[dx][0])
             def _():
-                main_copy(dx).start()
+                main_copy(dx, phase).start()
 
         @pl.when(phase == 0)
         def _():
@@ -317,24 +316,15 @@
             )
         table[t] = value
 
-    def close_half(dx):
-        @pl.when(has[dx][0])
-        def _():
-            main_arrival(dx).wait_recv()
-
-        first = 0 if dx < 0 else W
-        for t in range(first, first + W):
-            close(t)
-
-    @pl.when(upper_first == 0)
-    def _():
-        close_half(-1)
-        close_half(1)
-
-    @pl.when(upper_first == 1)
-    def _():
-        close_half(1)
-        close_half(-1)
+    for phase in range(2):
+        for dx in (-1, 1):
+            @pl.when(has[dx][0])
+            def _():
+                main_arrival(dx, phase).wait_recv()
+
+        for side in range(2):
+            for u in range(R):
+                close(side * block_x + R * phase + u)
 
     for k, (dx, dy) in enumerate(others):
         @pl.when(present(dx, dy))
@@ -343,7 +333,8 @@
     for dx in (-1, 1):
         @pl.when(has[dx][0])
         def _():
-            main_copy(dx).wait_send()
+            for phase in range(2):
+                main_copy(dx, phase).wait_send()
 
 
 def stack_levels(plain, matrices):
@@ -497,7 +488,7 @@
             pltpu.VMEM((2, 2, FOLD, LANES), F32),
             pltpu.VMEM((2, FOLD, LANES), F32),
             pltpu.VMEM((2, 2, FOLD, LANES), F32),
-            dma((particles // chunk,)), dma((4,)), dma((2,)), dma((2,)), dma((8,)), dma((8,)),
+            dma((particles // chunk,)), dma((4,)), dma((2, 2)), dma((2, 2)), dma((8,)), dma((8,)),
         ],
         compiler_params=pltpu.CompilerParams(
             collective_id=0, has_side_effects=True, vmem_limit_bytes=40 << 20

time: 16.5 us -> 16.6 us (level)
  no operation moved by 1% of the time
where the time goes in v8:
time: 16.6 us; the launch traced here: 16.4 us
  Pallas kernels  15.7 us (95%)
  between operations  0.69 us (4%)
    pallas_call x1, Pallas kernels, per_device(): pl.pallas_call(functools.partial(sums_kernel, counts, chunk, 512, block_x...  11 us
    pallas_call x1, Pallas kernels, per_device(): pl.pallas_call(functools.partial(react_kernel, block_x, block_y, piece, g...  4.76 us

profile of v8, /device:TPU:1, one launch (start us, length us, event | category | flops | bytes accessed | tf_op | source)
XLA Modules:
  0.0 16.4 jit_solution(16782656949345399241)
XLA Ops:
  0.6 0.0 copy-start.1
  0.6 0.0 copy-start
  0.7 0.0 copy-start.2
  0.7 11.0 %shard_map.95 = (f32[9,56,128]{2,1,0:T(8,128)S(1)}, f32[53,8192]{1,0:T(8,128)S(1)}, s32[2,8192]{1,0:T(2,128)S(1)}) custom-call(f32[53,8192]{1,0:T(8,128)} %comp.1, f32[1,8192]{1,0:T(1,128)} %bitcast.3, s32[2,8192]{1,0:T(2,128)} %cell_in.1, f32[53,4,128]{2,1,0:T(4,128)} %les_in.1, f32[4,128]{1,0:T(4,128)} %rate_in.1), custom_call_target="tpu_custom_call" | custom-call | tf_op jit(solution)/shard_map/pallas_call | solution.py:465
  11.6 0.0 copy-done.1
  11.7 0.0 copy-done
  11.7 0.0 copy-done.2
  11.7 4.8 %shard_map.96 = (f32[53,8192]{1,0:T(8,128)}, f32[53,4,128]{2,1,0:T(4,128)}) custom-call(f32[53,8192]{1,0:T(8,128)S(1)} %get-tuple-element.5.comp, s32[2,8192]{1,0:T(2,128)S(1)} %get-tuple-element.6.cell, s32[1,8192]{1,0:T(1,128)S(1)} %bitcast.2, f32[9,56,128]{2,1,0:T(8,128)S(1)} %get-tuple-element.7.table, f32[3,53,53]{2,1,0:T(8,128)S(1)} %copy-done, ...), custom_call_target="tpu_custom_call" | custom-call | tf_op jit(solution)/shard_map/pallas_call | solution.py:499
Async XLA Ops:
  0.6 11.0 %copy-start.1 = (f32[3,53,53]{2,1,0:T(8,128)S(1)}, f32[3,53,53]{2,1,0:T(8,128)}, u32[]{:S(2)}) copy-start(f32[3,53,53]{2,1,0:T(8,128)} %implicit.1) | copy-start | bytes 101128
  0.6 11.0 %copy-start = (f32[3,53,53]{2,1,0:T(8,128)S(1)}, f32[3,53,53]{2,1,0:T(8,128)}, u32[]{:S(2)}) copy-start(f32[3,53,53]{2,1,0:T(8,128)} %rate.1) | copy-start | bytes 101128
  0.7 11.0 %copy-start.2 = (s32[8192]{0:T(1024)S(1)}, s32[8192]{0:T(1024)}, u32[]{:S(2)}) copy-start(s32[8192]{0:T(1024)} %param.11) | copy-start | bytes 98308
